TPU v7x, 128 devices: a whole 4x4x4 slice. The times are simulated.
128 devices in a mesh: feat: 8 (over x_lo, y), dp: 16 (over z, x_hi, core).
Axes of the slice: x: 4 (x_hi: 2, x_lo: 2; x = x_hi * 2 + x_lo), y: 4, z: 4, core: 2. Of those that a mesh axis runs over, the one named last changes fastest.
Arguments:
- text_rows: bfloat16 [2048, 8192], P('dp', 'feat'), may hold values from -6 to 6
- q_weight: bfloat16 [8192, 8192], P(None, 'feat'), may hold values from -0.0625 to 0.0625
- features: bfloat16 [16, 1024, 7680], P('dp', None, 'feat'), may hold values from -6 to 6
- kv_weight: bfloat16 [7680, 2048], P('feat'), may hold values from -0.0625 to 0.0625
- q_gain: float32 [128], replicated, may hold values from 0.7 to 2.6
- k_gain: float32 [128], replicated, may hold values from 0.7 to 2.6
- attn_gate: float32 [1], replicated, may hold values from 0.5 to 2
- image_ids: int32 [256, 2], P('dp'), may hold values from 0 to 15, all different within a row; in each aligned block of 16 rows (0 to 15, 16 to 31, ...) at most 4 rows name the same one
- image_slot: int32 [16], replicated, may hold values from 0 to 15, each once
Outputs:
- attended: bfloat16 [2048, 8192], P('dp', 'feat')
Inputs may be any that keep to these rules, and one draw needn't show every extreme that they name: `image_ids`: each request names two different images; among the requests of one index of dp (aligned blocks of 16 requests) no image is named more than 4 times, a bound that some block reaches. Each position once; image i lies at position image_slot[i].
All inputs are finite; a program needn't handle non-finite values.
Results may differ from a plain program's by a relative error of at most 0.009.
The roundings to bfloat16 on the way count: a program that leaves them out, or rounds other values in their place, can miss the bound.
Values may be sent and summed in bfloat16 or wider, within the bound.
No kernel may reach another device: no remote copies, remote signals or barrier semaphores. Data moves between devices by JAX's collectives and lax.ppermute only.
A program may use at most 128 MiB of HBM per device.

v0:
```python
import jax
import jax.numpy as jnp
from jax import lax
from jax.sharding import PartitionSpec as P

epsilon = 1e-05


def head_norm(values, gain_vector):
    return (
        values
        * lax.rsqrt(jnp.mean(values * values, axis=-1, keepdims=True) + epsilon)
        * gain_vector
    )


def attend(queries, keyval, weights):
    head_width = queries.shape[-1]
    scores = jnp.einsum(
        "rhgd,hnd->rhgn", queries, keyval[..., :head_width], preferred_element_type=jnp.float32
    )
    exponent = jnp.exp(scores)
    exponent = exponent * weights[:, None, None, None]
    exponent = exponent.astype(jnp.bfloat16)
    denominator = jnp.sum(exponent.astype(jnp.float32), axis=-1)
    numerator = jnp.einsum(
        "rhgn,hnd->rhgd", exponent, keyval[..., head_width:], preferred_element_type=jnp.float32
    )
    return (numerator, denominator)


def per_device(
    text_rows, q_weight, features, kv_weight, q_gain, k_gain, attn_gate, image_ids, image_slot
):
    row_count = text_rows.shape[0]
    requests = image_ids.shape[0]
    text_words = row_count // requests
    head_width = q_gain.shape[0]
    heads_all = kv_weight.shape[1] // (2 * head_width)
    kv_local = heads_all // lax.axis_size("feat")
    group_size = q_weight.shape[1] // (head_width * kv_local)
    weight_block = q_weight
    queries = jnp.dot(
        lax.all_gather(text_rows, "feat", axis=1, tiled=True),
        weight_block,
        preferred_element_type=jnp.float32,
    )
    queries = head_norm(
        queries.reshape(row_count, kv_local, group_size, head_width), q_gain
    ) * head_width ** (-0.5)
    queries = queries.astype(jnp.bfloat16)
    kv_table = kv_weight.reshape(kv_weight.shape[0], heads_all, 2 * head_width)
    vision_rows = features[0]
    weight_block = kv_table
    summed = lax.psum_scatter(
        jnp.einsum("nf,fhc->hnc", vision_rows, weight_block, preferred_element_type=jnp.float32),
        "feat",
        scatter_dimension=0,
        tiled=True,
    )
    normed_keys = head_norm(summed[..., :head_width], k_gain)
    keyval = jnp.concatenate([normed_keys, summed[..., head_width:]], axis=-1).astype(jnp.bfloat16)
    image_count = image_slot.shape[0]
    matches = image_ids[:, :, None] == jnp.arange(image_count, dtype=jnp.int32)[None, None, :]
    owners = jnp.sum(jnp.where(matches, image_slot[None, None, :], 0), axis=-1)
    starting = (
        jnp.zeros((row_count, kv_local, group_size, head_width), jnp.float32),
        jnp.zeros((row_count, kv_local, group_size), jnp.float32),
    )
    shard_piece = lax.all_gather(keyval[None], "dp", axis=0, tiled=True)

    def add_one(position, partial_sums):
        reads_image = jnp.any(owners == position, axis=1)
        weights = jnp.repeat(reads_image.astype(jnp.float32), text_words)
        kv_block = lax.dynamic_index_in_dim(shard_piece, position, 0, keepdims=False)
        numerator, denominator = attend(queries, kv_block, weights)
        return (partial_sums[0] + numerator, partial_sums[1] + denominator)

    numerator, denominator = lax.fori_loop(0, shard_piece.shape[0], add_one, starting)
    result = numerator / denominator[..., None]
    return (jnp.tanh(attn_gate[0]) * result).astype(jnp.bfloat16).reshape(row_count, -1)


def solution(mesh):
    in_specs = (
        P("dp", "feat"),
        P(None, "feat"),
        P("dp", None, "feat"),
        P("feat", None),
        P(),
        P(),
        P(),
        P("dp", None),
        P(),
    )
    out_specs = P("dp", "feat")
    return jax.shard_map(
        per_device, mesh=mesh, in_specs=in_specs, out_specs=out_specs, check_vma=False
    )
```

profile of v0, /device:TPU:1, one launch (start us, length us, event | category | flops | bytes accessed | tf_op | source)
XLA Modules:
  0.0 329.7 jit_solution(1036196203318548550)
XLA Ops:
  6.5 1.5 copy-done
  8.1 9.0 %fusion.13 = f32[8,1024,256]{1,2,0:T(8,128)} fusion(bf16[120,8,8,256]{3,2,1,0:T(8,128)(2,1)} %bitcast.86, bf16[1,1024,960]{1,2,0:T(8,128)(2,1)S(1)} %copy-done), kind=kOutput, calls=%fused_computation.16 | convolution fusion | flops 4026531840 | bytes 14286848 | tf_op jit(solution)/shard_map/nf,fhc->hnc/dot_general | solution.py:56
  17.2 0.7 all-gather.5.cloned.1.call-update
  17.9 95.3 %reduce-scatter.2.cloned.1.call-done = f32[1,1024,256]{1,2,0:T(8,128)} async-done(((f32[8,1024,256]{1,2,0:T(8,128)}), f32[1,1024,256]{1,2,0:T(8,128)}) %reduce-scatter.2.cloned.1.call-update) | async-done | bytes 1048592 | tf_op jit(solution)/shard_map/reduce_scatter | solution.py:55
  113.2 1.1 multiply_reduce_fusion.1
  114.3 1.1 fusion.21
  115.4 1.1 fusion.20
  116.6 1.0 copy.42
  118.4 0.2 select_reduce_fusion
  118.5 31.4 %all-gather.5.cloned.1.call-done = bf16[128,8192]{1,0:T(8,128)(2,1)} async-done(((bf16[128,1024]{1,0:T(8,128)(2,1)}), bf16[128,8192]{1,0:T(8,128)(2,1)}) %all-gather.5.cloned.1.call-update) | async-done | bytes 2097168 | tf_op jit(solution)/shard_map/all_gather | solution.py:44
  149.9 8.7 %convolution_bitcast_fusion = f32[16,8,8,128]{3,1,2,0:T(8,128)S(1)} fusion(bf16[128,8192]{1,0:T(8,128)(2,1)} %all-gather.5.cloned.1.call-done, bf16[8192,1024]{1,0:T(8,128)(2,1)} %param.12), kind=kOutput, calls=%fused_computation.18 | convolution fusion | flops 2147483648 | bytes 19398656 | tf_op jit(solution)/shard_map/dot_general | solution.py:43
  158.7 0.2 multiply_reduce_fusion
  159.0 0.2 fusion.19
  159.3 71.2 %all-gather.3.cloned.1.call-done = bf16[16,1,1024,256]{3,2,1,0:T(8,128)(2,1)} async-done(((bf16[1,1,1024,256]{3,2,1,0:T(8,128)(2,1)}), bf16[16,1,1024,256]{3,2,1,0:T(8,128)(2,1)}) %all-gather.3.cloned.1.call-update) | async-done | bytes 8388624 | tf_op jit(solution)/shard_map/all_gather | solution.py:70
  230.5 91.7 %while.16 = (s32[]{:T(128)}, f32[128,1,8,128]{0,3,2,1:T(8,128)S(1)}, f32[128,1,8]{0,2,1:T(8,128)S(1)}, bf16[16,1,1024,256]{3,2,1,0:T(8,128)(2,1)}, bf16[128,1,8,...) while((s32[]{:T(128)}, f32[128,1,8,128]{0,3,2,1:T(8,128)S(1)}, ...), condition=%wide.region_7.8_spmd.clone, body=%wide.region_4.7_spmd.clone.sunk | while | flops 541328448 | bytes 7096712 | solution.py:79
  230.5 1.1 dynamic-slice_bitcast_fusion.2
  231.8 2.3 convert_reduce_fusion.2
  234.1 2.1 fusion.27
  236.2 1.1 dynamic-slice_bitcast_fusion.2
  237.5 2.3 convert_reduce_fusion.2
  239.8 2.1 fusion.27
  242.0 1.1 dynamic-slice_bitcast_fusion.2
  243.2 2.3 convert_reduce_fusion.2
  245.5 2.1 fusion.27
  247.7 1.1 dynamic-slice_bitcast_fusion.2
  249.0 2.3 convert_reduce_fusion.2
  251.3 2.1 fusion.27
  253.4 1.1 dynamic-slice_bitcast_fusion.2
  254.7 2.3 convert_reduce_fusion.2
  257.0 2.1 fusion.27
  259.2 1.1 dynamic-slice_bitcast_fusion.2
  260.4 2.3 convert_reduce_fusion.2
  262.7 2.1 fusion.27
  264.9 1.1 dynamic-slice_bitcast_fusion.2
  266.2 2.3 convert_reduce_fusion.2
  268.5 2.1 fusion.27
  270.6 1.1 dynamic-slice_bitcast_fusion.2
  271.9 2.3 convert_reduce_fusion.2
  274.2 2.1 fusion.27
  276.4 1.1 dynamic-slice_bitcast_fusion.2
  277.6 2.3 convert_reduce_fusion.2
  279.9 2.1 fusion.27
  282.1 1.1 dynamic-slice_bitcast_fusion.2
  283.4 2.3 convert_reduce_fusion.2
  285.7 2.1 fusion.27
  287.8 1.1 dynamic-slice_bitcast_fusion.2
  289.1 2.3 convert_reduce_fusion.2
  291.4 2.1 fusion.27
  293.6 1.1 dynamic-slice_bitcast_fusion.2
  294.9 2.3 convert_reduce_fusion.2
  297.1 2.1 fusion.27
  299.3 1.1 dynamic-slice_bitcast_fusion.2
  300.6 2.3 convert_reduce_fusion.2
  302.9 2.1 fusion.27
  305.0 1.1 dynamic-slice_bitcast_fusion.2
  306.3 2.3 convert_reduce_fusion.2
  308.6 2.1 fusion.27
  310.8 1.1 dynamic-slice_bitcast_fusion.2
  312.1 2.3 convert_reduce_fusion.2
  314.3 2.1 fusion.27
  316.5 1.1 dynamic-slice_bitcast_fusion.2
  317.8 2.3 convert_reduce_fusion.2
  320.1 2.1 fusion.27
  322.3 0.9 copy.48
  (102 shorter events, 3.6 us)
Async XLA Ops:
  6.5 1.5 copy-start
  6.5 106.6 %reduce-scatter.2.cloned.1.call-start = ((), (), s32[]{:S(2)}) async-start(), calls=%async_computation.1 | async-start | bytes 9437184 | tf_op jit(solution)/shard_map/reduce_scatter | solution.py:55
  17.1 98.3 %copy-start.3 = (f32[128]{0:T(128)S(1)}, f32[128]{0:T(128)}, u32[]{:S(2)}) copy-start(f32[128]{0:T(128)} %param.16) | copy-start | bytes 1540
  17.1 101.2 %copy-start.1 = (s32[16,2]{0,1:T(2,128)S(1)}, s32[16,2]{0,1:T(2,128)}, u32[]{:S(2)}) copy-start(s32[16,2]{0,1:T(2,128)} %param.18) | copy-start | bytes 388
  17.1 101.2 %copy-start.2 = (s32[16]{0:T(128)S(1)}, s32[16]{0:T(128)}, u32[]{:S(2)}) copy-start(s32[16]{0:T(128)} %param.19) | copy-start | bytes 196
  17.1 132.8 %all-gather.5.cloned.1.call-start = ((), (), s32[]{:S(2)}) async-start(), calls=%async_computation.3 | async-start | bytes 2359296 | tf_op jit(solution)/shard_map/all_gather | solution.py:44
  17.9 212.6 %all-gather.3.cloned.1.call-start = ((), (), s32[]{:S(2)}) async-start(), calls=%async_computation.2 | async-start | bytes 8912896 | tf_op jit(solution)/shard_map/all_gather | solution.py:70
  118.5 40.5 %copy-start.4 = (f32[128]{0:T(128)S(1)}, f32[128]{0:T(128)}, u32[]{:S(2)}) copy-start(f32[128]{0:T(128)} %param.15) | copy-start | bytes 1540
Sparse Core Ops, SparseCore 0:
  17.2 95.9 reduce-scatter.1
  114.8 35.0 all-gather.4
  152.4 78.0 all-gather.2
where the time goes:
time: 331 us; the launch traced here: 330 us
  waiting for transfers between devices  199 us (60%)
  matrix products  88.4 us (27%)
  local copies, waits for them, and re-layouts  24.5 us (7%)
  between operations  13.9 us (4%)
  other arithmetic  3.55 us (1%)
    reduce_scatter x1, waiting for transfers between devices, per_device(): lax.psum_scatter(jnp.einsum('nf,fhc->hnc', vision_rows, weight_block, pre...  95.3 us
    all_gather x1, waiting for transfers between devices, per_device(): shard_piece = lax.all_gather(keyval[None], 'dp', axis=0, tiled=True)  71.2 us
    dot_general x16, matrix products, attend(): jnp.einsum('rhgd,hnd->rhgn', queries, keyval[..., :head_width], preferred...  36.6 us
    dot_general x16, matrix products, attend(): jnp.einsum('rhgn,hnd->rhgd', exponent, keyval[..., head_width:], preferre...  34.2 us
    all_gather x1, waiting for transfers between devices, per_device(): lax.all_gather(text_rows, 'feat', axis=1, tiled=True)  31.4 us
    squeeze x16, local copies, waits for them, and re-layouts, add_one(): lax.dynamic_index_in_dim(shard_piece, position, 0, keepdims=False)  17.3 us
    dot_general x1, matrix products, per_device(): jnp.einsum('nf,fhc->hnc', vision_rows, weight_block, preferred_element_ty...  8.98 us
    dot_general x1, matrix products, per_device(): jnp.dot(lax.all_gather(text_rows, 'feat', axis=1, tiled=True), weight_blo...  8.74 us
  transfers between devices with their start and end apart: 3, of which 3 were waited for; matrix products, arithmetic and copies ran while one was open for 4% of the time, Pallas kernels for 0%

commit v1 on v0

v1 whole, which is shorter than its diff:
```python
import functools

import jax
import jax.numpy as jnp
from jax import lax
from jax.experimental import pallas as pl
from jax.experimental.pallas import tpu as pltpu
from jax.sharding import PartitionSpec as P

epsilon = 1e-05
CAP = 4


def attend_kernel(q_ref, key_ref, value_ref, num_ref, den_ref):
    head = pl.program_id(0)
    scores = jnp.dot(q_ref[...], key_ref[...], preferred_element_type=jnp.float32)
    exponent = jnp.exp(scores).astype(jnp.bfloat16)
    width = num_ref.shape[1]
    both = jnp.dot(exponent, value_ref[...], preferred_element_type=jnp.float32)
    num_ref[...] = both[:, :width].astype(num_ref.dtype)
    total = both[:, width:]
    coarse = total.astype(jnp.bfloat16)
    fine = (total - coarse.astype(jnp.float32)).astype(jnp.bfloat16)
    lane = lax.broadcasted_iota(jnp.int32, total.shape, 1)
    heads = pl.num_programs(0)
    packed = jnp.where(
        lane == head,
        coarse.astype(jnp.float32),
        jnp.where(lane == head + heads, fine.astype(jnp.float32), 0.0),
    )

    @pl.when(head == 0)
    def _():
        den_ref[...] = jnp.zeros_like(den_ref)

    den_ref[...] += packed.astype(jnp.bfloat16)


def attend(queries, keys, values):
    rows, columns = queries.shape
    width, count = keys.shape
    heads = columns // width
    extended = jnp.concatenate([values, jnp.ones_like(values)], axis=1)
    return pl.pallas_call(
        attend_kernel,
        grid=(heads,),
        in_specs=[
            pl.BlockSpec((rows, width), lambda h: (0, h)),
            pl.BlockSpec((width, count), lambda h: (0, 0)),
            pl.BlockSpec((count, 2 * width), lambda h: (0, 0)),
        ],
        out_specs=[
            pl.BlockSpec((rows, width), lambda h: (0, h)),
            pl.BlockSpec((rows, width), lambda h: (0, 0)),
        ],
        out_shape=[
            jax.ShapeDtypeStruct((rows, columns), jnp.bfloat16),
            jax.ShapeDtypeStruct((rows, width), jnp.bfloat16),
        ],
        compiler_params=pltpu.CompilerParams(vmem_limit_bytes=40 << 20),
        name="attend",
    )(queries, keys, extended)


def slot_table(image_ids, image_slot, text_words):
    count = image_slot.shape[0]
    requests = image_ids.shape[0]
    matches = image_ids[:, :, None] == jnp.arange(count, dtype=jnp.int32)[None, None, :]
    owners = jnp.sum(jnp.where(matches, image_slot[None, None, :], 0), axis=-1)
    named = jnp.any(owners[:, :, None] == jnp.arange(count, dtype=jnp.int32), axis=1)
    earlier = jnp.arange(requests)[:, None] > jnp.arange(requests)[None, :]
    rank = jnp.sum(jnp.where(earlier[:, :, None], named[None].astype(jnp.int32), 0), axis=1)
    place = jnp.where(named, rank, CAP)
    picks = place.T[:, None, :] == jnp.arange(CAP, dtype=jnp.int32)[None, :, None]
    same = jnp.arange(text_words)[:, None] == jnp.arange(text_words)[None, :]
    table = picks[:, :, None, :, None] & same[None, None, :, None, :]
    return table.astype(jnp.bfloat16).reshape(
        count * CAP * text_words, requests * text_words
    )


def per_device(
    text_rows, q_weight, features, kv_weight, q_gain, k_gain, attn_gate, image_ids, image_slot
):
    rows = text_rows.shape[0]
    requests = image_ids.shape[0]
    words = rows // requests
    images = image_slot.shape[0]
    width = q_gain.shape[0]
    columns = q_weight.shape[1]
    group = columns // width
    heads_all = kv_weight.shape[1] // (2 * width)

    table = kv_weight.reshape(kv_weight.shape[0], heads_all, 2 * width)
    partial = jnp.einsum("nf,fhc->hcn", features[0], table, preferred_element_type=jnp.float32)
    parts = lax.all_to_all(partial.astype(jnp.bfloat16), "feat", 0, 0, tiled=True)
    summed = jnp.sum(parts.astype(jnp.float32), axis=0)
    key = summed[:width]
    key = key * lax.rsqrt(jnp.mean(key * key, axis=0, keepdims=True) + epsilon) * k_gain[:, None]
    key = key.astype(jnp.bfloat16)
    value = summed[width:].astype(jnp.bfloat16).T

    picks = slot_table(image_ids, image_slot, words)
    text = lax.all_gather(text_rows, "feat", axis=1, tiled=True)
    queries = jnp.dot(text, q_weight, preferred_element_type=jnp.float32)
    queries = queries.reshape(rows, group, width)
    queries = (
        queries
        * lax.rsqrt(jnp.mean(queries * queries, axis=-1, keepdims=True) + epsilon)
        * q_gain
        * width ** (-0.5)
    )
    queries = queries.astype(jnp.bfloat16).reshape(rows, columns)
    sent = jnp.dot(picks, queries, preferred_element_type=jnp.float32).astype(jnp.bfloat16)
    arrived = lax.all_to_all(
        sent.reshape(images, CAP * words, columns), "dp", 0, 0, tiled=True
    ).reshape(images * CAP * words, columns)

    numerator, denominator = attend(arrived, key, value)
    back = jnp.concatenate([numerator, denominator], axis=1)
    back = lax.all_to_all(
        back.reshape(images, CAP * words, columns + width), "dp", 0, 0, tiled=True
    ).reshape(images * CAP * words, columns + width)
    both = lax.dot_general(
        picks, back, (((0,), (0,)), ((), ())), preferred_element_type=jnp.float32
    )
    total = both[:, columns : columns + group] + both[:, columns + group : columns + 2 * group]
    result = both[:, :columns].reshape(rows, group, width) / total[:, :, None]
    return (jnp.tanh(attn_gate[0]) * result).astype(jnp.bfloat16).reshape(rows, columns)


def solution(mesh):
    in_specs = (
        P("dp", "feat"),
        P(None, "feat"),
        P("dp", None, "feat"),
        P("feat", None),
        P(),
        P(),
        P(),
        P("dp", None),
        P(),
    )
    return jax.shard_map(
        per_device, mesh=mesh, in_specs=in_specs, out_specs=P("dp", "feat"), check_vma=False
    )
```

time: 331 us -> 170 us (0.51)
  waiting for transfers between devices: 199 us -> 93.2 us
  matrix products: 88.4 us -> 19 us
  starting transfers between devices: 0.08 us -> 18.2 us
  local copies, waits for them, and re-layouts: 24.5 us -> 7.58 us
  Pallas kernels: 0 us -> 7.43 us
  other arithmetic: 3.55 us -> 9.31 us
    reduce_scatter x1 -> x0, waiting for transfers between devices: 95.3 us -> none  [per_device(): lax.psum_scatter(jnp.einsum('nf,fhc->hnc', vision_rows, weight_block, pre...]
    dot_general x34 -> x4, matrix products: 88.4 us -> 19 us  [the longest x1 8.73 us: per_device(): queries = jnp.dot(text, q_weight, preferred_element_type=jnp.float32)]
    all_gather x2 -> x1, waiting for transfers between devices: 103 us -> 66.2 us  [per_device(): text = lax.all_gather(text_rows, 'feat', axis=1, tiled=True)]
    all_to_all x0 -> x3, waiting for transfers between devices: none -> 26.3 us  [the longest x1 18 us: per_device(): lax.all_to_all(back.reshape(images, CAP * words, columns + width), 'dp',...]
    all_to_all x0 -> x3, starting transfers between devices: none -> 18.2 us  [the longest x1 7.72 us: per_device(): lax.all_to_all(sent.reshape(images, CAP * words, columns), 'dp', 0, 0, ti...]
    squeeze x16 -> x0, local copies, waits for them, and re-layouts: 17.3 us -> none  [add_one(): lax.dynamic_index_in_dim(shard_piece, position, 0, keepdims=False)]
    pallas_call x0 -> x1, Pallas kernels: none -> 7.43 us  [attend(): pl.pallas_call(attend_kernel, grid=(heads,), in_specs=[pl.BlockSpec((rows...]
  transfers between devices with their start and end apart: 3 -> 4, of which waited for: 3 -> 3; matrix products, arithmetic and copies ran while one was open for 4% -> 18% of each run, Pallas kernels for 0% -> 0%
where the time goes in v1:
time: 170 us; the launch traced here: 169 us
  waiting for transfers between devices  93.2 us (55%)
  matrix products  19 us (11%)
  starting transfers between devices  18.2 us (11%)
  between operations  14.3 us (8%)
  other arithmetic  9.31 us (5%)
  local copies, waits for them, and re-layouts  7.58 us (4%)
  Pallas kernels  7.43 us (4%)
    all_gather x1, waiting for transfers between devices, per_device(): text = lax.all_gather(text_rows, 'feat', axis=1, tiled=True)  66.2 us
    all_to_all x1, waiting for transfers between devices, per_device(): lax.all_to_all(back.reshape(images, CAP * words, columns + width), 'dp',...  18 us
    dot_general x1, matrix products, per_device(): queries = jnp.dot(text, q_weight, preferred_element_type=jnp.float32)  8.73 us
    dot_general x1, matrix products, per_device(): jnp.einsum('nf,fhc->hcn', features[0], table, preferred_element_type=jnp....  8.36 us
    all_to_all x1, waiting for transfers between devices, per_device(): lax.all_to_all(sent.reshape(images, CAP * words, columns), 'dp', 0, 0, ti...  8.23 us
    all_to_all x1, starting transfers between devices, per_device(): lax.all_to_all(sent.reshape(images, CAP * words, columns), 'dp', 0, 0, ti...  7.72 us
    pallas_call x1, Pallas kernels, attend(): pl.pallas_call(attend_kernel, grid=(heads,), in_specs=[pl.BlockSpec((rows...  7.43 us
    all_to_all x1, starting transfers between devices, per_device(): lax.all_to_all(partial.astype(jnp.bfloat16), 'feat', 0, 0, tiled=True)  6.08 us
  transfers between devices with their start and end apart: 4, of which 3 were waited for; matrix products, arithmetic and copies ran while one was open for 18% of the time, Pallas kernels for 0%

profile of v1, /device:TPU:1, one launch (start us, length us, event | category | flops | bytes accessed | tf_op | source)
XLA Modules:
  0.0 169.0 jit_solution(9780607244963820722)
XLA Ops:
  6.5 0.0 copy-start
  6.5 0.0 all-gather.2.cloned.1.call-start
  6.5 0.7 all-gather.2.cloned.1.call-update
  7.3 0.8 copy-done
  8.1 8.4 %fusion.3 = bf16[8,256,1024]{2,1,0:T(8,128)(2,1)} fusion(bf16[120,8,8,256]{3,2,1,0:T(8,128)(2,1)} %bitcast.57, bf16[1,1024,960]{1,2,0:T(8,128)(2,1)S(1)} %copy-done), kind=kOutput, calls=%fused_computation.4 | convolution fusion | flops 4028628992 | bytes 10092544 | tf_op jit(solution)/shard_map/nf,fhc->hcn/dot_general | solution.py:95
  16.4 0.0 copy-start.5
  16.4 0.0 copy-start.6
  16.4 0.0 copy-start.7
  16.4 6.1 %all-to-all-start.1 = ((bf16[8,256,1024]{2,1,0:T(8,128)(2,1)}), bf16[8,256,1024]{2,1,0:T(8,128)(2,1)}, u32[]{:S(2)}, u32[]{:S(2)}) async-start(bf16[8,256,1024]{2,1,0:T(8,128)(2,1)} %fusion.3), calls=%async_computation.1 | async-start | bytes 8388608 | tf_op jit(solution)/shard_map/all_to_all | solution.py:96
  22.5 0.0 copy-done.5
  22.5 0.0 copy-done.6
  22.5 0.2 select_reduce_fusion.1
  22.7 0.1 fusion.15
  22.8 0.1 select_reduce_fusion
  23.0 0.1 copy.29
  23.1 0.5 broadcast_and_fusion
  23.6 2.2 %and.27 = pred[512,128]{1,0:T(32,128)(4,1)S(1)} reshape(pred[16,4,8,16,8]{4,3,2,1,0:T(8,128)(4,1)S(1)} %broadcast_and_fusion) | data formatting | bytes 131072 | tf_op jit(solution)/shard_map/and | solution.py:76
  25.8 0.0 copy-done.7
  25.8 0.0 copy-start.3
  25.8 66.2 %all-gather.2.cloned.1.call-done = bf16[128,8192]{1,0:T(8,128)(2,1)} async-done(((bf16[128,1024]{1,0:T(8,128)(2,1)}), bf16[128,8192]{1,0:T(8,128)(2,1)}) %all-gather.2.cloned.1.call-update) | async-done | bytes 2097168 | tf_op jit(solution)/shard_map/all_gather | solution.py:104
  92.1 8.7 %fusion.17 = f32[128,1024]{1,0:T(8,128)S(1)} fusion(bf16[128,8192]{1,0:T(8,128)(2,1)} %all-gather.2.cloned.1.call-done, bf16[8192,1024]{1,0:T(8,128)(2,1)} %param.10), kind=kOutput, calls=%fused_computation.36 | convolution fusion | flops 2147483648 | bytes 19398656 | tf_op jit(solution)/shard_map/dot_general | solution.py:105
  100.9 0.1 copy.36
  101.0 0.2 reduce_sum.47
  101.2 0.1 copy.31
  101.4 0.2 mul.66
  101.6 0.0 copy-done.3
  101.6 1.5 convolution_convert_fusion
  103.1 0.0 all-to-all-done.1
  103.1 7.7 %all-to-all-start = ((bf16[16,32,1024]{2,1,0:T(8,128)(2,1)}), bf16[16,32,1024]{2,1,0:T(8,128)(2,1)S(1)}, u32[]{:S(2)}, u32[]{:S(2)}) async-start(bf16[16,32,1024]{2,1,0:T(8,128)(2,1)} %bitcast.52), calls=%async_computation | async-start | bytes 2097152 | tf_op jit(solution)/shard_map/all_to_all | solution.py:115
  110.8 3.2 %convert_reduce_fusion = f32[256,1024]{1,0:T(8,128)S(1)} fusion(bf16[8,256,1024]{2,1,0:T(8,128)(2,1)} %all-to-all-done.1), kind=kLoop, calls=%fused_computation | loop fusion | flops 3932160 | bytes 5242880 | tf_op jit(solution)/shard_map/reduce_sum | solution.py:97
  114.0 0.0 copy-start.2
  114.0 1.0 copy-done.2
  115.0 0.0 copy-start.8
  115.0 0.8 copy.34
  115.9 1.0 concatenate.6.value_ref
  116.9 1.1 multiply_reduce_fusion
  118.0 0.0 copy-done.8
  118.0 1.8 %multiply_convert_fusion.key_ref = bf16[128,1024]{1,0:T(8,128)(2,1)} fusion(f32[256,1024]{1,0:T(8,128)} %copy-done.2, f32[128]{0:T(128)S(1)} %copy-done.8, f32[1024]{0:T(1024)S(1)} %add_rsqrt_fusion), kind=kLoop, calls=%fused_computation.16 | loop fusion | flops 393216 | bytes 791040 | tf_op jit(solution)/shard_map/convert_element_type | solution.py:100
  119.8 8.2 %all-to-all-done = bf16[16,32,1024]{2,1,0:T(8,128)(2,1)S(1)} async-done(((bf16[16,32,1024]{2,1,0:T(8,128)(2,1)}), bf16[16,32,1024]{2,1,0:T(8,128)(2,1)S(1)}, u32[]{:S(2)}, u32[]{:S(2)}) %all-to-all-start) | async-done | bytes 1048608 | tf_op jit(solution)/shard_map/all_to_all | solution.py:115
  128.0 0.0 copy-start.1
  128.1 0.9 copy-done.1
  129.0 7.4 %attend.1 = (bf16[512,1024]{1,0:T(8,128)(2,1)S(1)}, bf16[512,128]{1,0:T(8,128)(2,1)S(1)}) custom-call(bf16[512,1024]{1,0:T(8,128)(2,1)S(1)} %bitcast.49, bf16[128,1024]{1,0:T(8,128)(2,1)S(1)} %copy-done.1, bf16[1024,256]{1,0:T(8,128)(2,1)S(1)} %concatenate.6.value_ref), custom_call_target="tpu_custom_call" | custom-call | tf_op jit(solution)/shard_map/attend/pallas_call | solution.py:44
  136.4 0.0 copy-start.4
  136.4 1.1 pad_maximum_fusion
  137.5 4.4 %all-to-all-start.2 = ((bf16[16,32,1152]{2,1,0:T(8,128)(2,1)}), bf16[16,32,1152]{2,1,0:T(8,128)(2,1)S(1)}, u32[]{:S(2)}, u32[]{:S(2)}) async-start(bf16[16,32,1152]{2,1,0:T(8,128)(2,1)} %bitcast.51), calls=%async_computation.2 | async-start | bytes 2359296 | tf_op jit(solution)/shard_map/all_to_all | solution.py:121
  142.6 18.0 %all-to-all-done.2 = bf16[16,32,1152]{2,1,0:T(8,128)(2,1)S(1)} async-done(((bf16[16,32,1152]{2,1,0:T(8,128)(2,1)}), bf16[16,32,1152]{2,1,0:T(8,128)(2,1)S(1)}, u32[]{:S(2)}, u32[]{:S(2)}) %all-to-all-start.2) | async-done | bytes 1179680 | tf_op jit(solution)/shard_map/all_to_all | solution.py:121
  160.7 0.0 copy-done.4
  160.7 0.4 fusion.18
  161.1 0.1 slice_add_fusion
  161.2 0.2 div.27
  161.3 0.8 fusion.8
  (11 shorter events, 0.2 us)
Async XLA Ops:
  6.5 1.5 copy-start
  6.5 85.5 %all-gather.2.cloned.1.call-start = ((), (), s32[]{:S(2)}) async-start(), calls=%async_computation.3 | async-start | bytes 2359296 | tf_op jit(solution)/shard_map/all_gather | solution.py:104
  16.4 6.1 %copy-start.5 = (s32[16,2]{0,1:T(2,128)S(1)}, s32[16,2]{0,1:T(2,128)}, u32[]{:S(2)}) copy-start(s32[16,2]{0,1:T(2,128)} %param.16) | copy-start | bytes 388
  16.4 6.1 %copy-start.6 = (s32[16]{0:T(128)S(1)}, s32[16]{0:T(128)}, u32[]{:S(2)}) copy-start(s32[16]{0:T(128)} %param.17) | copy-start | bytes 196
  16.4 9.4 %copy-start.7 = (f32[128]{0:T(128)S(1)}, f32[128]{0:T(128)}, u32[]{:S(2)}) copy-start(f32[128]{0:T(128)} %param.13) | copy-start | bytes 1540
  16.4 86.7 %all-to-all-start.1 = ((bf16[8,256,1024]{2,1,0:T(8,128)(2,1)}), bf16[8,256,1024]{2,1,0:T(8,128)(2,1)}, u32[]{:S(2)}, u32[]{:S(2)}) async-start(bf16[8,256,1024]{2,1,0:T(8,128)(2,1)} %fusion.3), calls=%async_computation.1 | async-start | bytes 8388608 | tf_op jit(solution)/shard_map/all_to_all | solution.py:96
  25.8 75.8 %copy-start.3 = (pred[512,128]{1,0:T(32,128)(4,1)}, pred[512,128]{1,0:T(32,128)(4,1)S(1)}, u32[]{:S(2)}) copy-start(pred[512,128]{1,0:T(32,128)(4,1)S(1)} %and.27) | copy-start | bytes 196612
  103.1 24.9 %all-to-all-start = ((bf16[16,32,1024]{2,1,0:T(8,128)(2,1)}), bf16[16,32,1024]{2,1,0:T(8,128)(2,1)S(1)}, u32[]{:S(2)}, u32[]{:S(2)}) async-start(bf16[16,32,1024]{2,1,0:T(8,128)(2,1)} %bitcast.52), calls=%async_computation | async-start | bytes 2097152 | tf_op jit(solution)/shard_map/all_to_all | solution.py:115
  114.0 1.0 copy-start.2
  115.0 3.0 %copy-start.8 = (f32[128]{0:T(128)S(1)}, f32[128]{0:T(128)}, u32[]{:S(2)}) copy-start(f32[128]{0:T(128)} %param.14) | copy-start | bytes 1540
  128.0 1.0 copy-start.1
  136.4 24.2 %copy-start.4 = (pred[512,128]{1,0:T(32,128)(4,1)S(1)}, pred[512,128]{1,0:T(32,128)(4,1)}, u32[]{:S(2)}) copy-start(pred[512,128]{1,0:T(32,128)(4,1)} %copy-done.3) | copy-start | bytes 196612
  137.5 23.1 %all-to-all-start.2 = ((bf16[16,32,1152]{2,1,0:T(8,128)(2,1)}), bf16[16,32,1152]{2,1,0:T(8,128)(2,1)S(1)}, u32[]{:S(2)}, u32[]{:S(2)}) async-start(bf16[16,32,1152]{2,1,0:T(8,128)(2,1)} %bitcast.51), calls=%async_computation.2 | async-start | bytes 2359296 | tf_op jit(solution)/shard_map/all_to_all | solution.py:121
Sparse Core Ops, SparseCore 0:
  9.0 83.0 all-gather.1

commit v2 on v0

v2 whole, which is shorter than its diff:
```python
import functools

import jax
import jax.numpy as jnp
from jax import lax
from jax.experimental import pallas as pl
from jax.experimental.pallas import tpu as pltpu
from jax.sharding import PartitionSpec as P

epsilon = 1e-05
CAP = 4
RING = 4
KEY_SCALE = 64.0


def permute(values, across, along):
    pairs = [
        (side * RING + place, (side ^ across) * RING + (place + along) % RING)
        for side in range(2)
        for place in range(RING)
    ]
    return lax.ppermute(values, "feat", pairs)


def project_kernel(_, *refs):
    weights, (vision_ref, key_ref, value_ref) = refs[: 2 * RING], refs[2 * RING :]
    for part, out_ref in enumerate((key_ref, value_ref)):
        weight = jnp.concatenate([w[...] for w in weights[part::2]], axis=1)
        product = lax.dot_general(
            weight, vision_ref[...], (((0,), (0,)), ((), ())), preferred_element_type=jnp.float32
        )
        out_ref[...] = product.reshape(out_ref.shape).astype(out_ref.dtype)


def project(heads, kv_weight, vision, width, value_type):
    depth, tokens = vision.shape
    specs = [
        pl.BlockSpec((depth, width), functools.partial(lambda j, part, g, h: (0, 2 * h[j] + part), j, part))
        for j in range(RING)
        for part in range(2)
    ]
    out = pl.BlockSpec((RING, width, tokens), lambda g, h: (0, 0, 0))
    return pl.pallas_call(
        project_kernel,
        grid_spec=pltpu.PrefetchScalarGridSpec(
            num_scalar_prefetch=1,
            grid=(1,),
            in_specs=specs + [pl.BlockSpec((depth, tokens), lambda g, h: (0, 0))],
            out_specs=[out, out],
        ),
        out_shape=[
            jax.ShapeDtypeStruct((RING, width, tokens), jnp.float32),
            jax.ShapeDtypeStruct((RING, width, tokens), value_type),
        ],
        compiler_params=pltpu.CompilerParams(vmem_limit_bytes=24 << 20),
        name="project",
    )(heads, *([kv_weight] * (2 * RING)), vision)


def query_step_kernel(blocks, text_ref, weight_ref, *refs):
    total_ref, block_ref, sems = refs[-3:]
    count, _, depth = text_ref.shape
    copies = [
        pltpu.make_async_copy(
            weight_ref.at[pl.ds(pl.multiple_of(blocks[i] * depth, depth), depth)],
            block_ref.at[i],
            sems.at[i],
        )
        for i in range(count)
    ]
    for copy in copies:
        copy.start()
    total = refs[0][...] if len(refs) == 4 else None
    for i, copy in enumerate(copies):
        copy.wait()
        product = jnp.dot(text_ref[i], block_ref[i], preferred_element_type=jnp.float32)
        total = product if total is None else total + product
    total_ref[...] = total


def query_step(blocks, texts, weight, total=None):
    count, rows, depth = texts.shape
    columns = weight.shape[1]
    vmem = pl.BlockSpec(memory_space=pltpu.VMEM)
    return pl.pallas_call(
        query_step_kernel,
        grid_spec=pltpu.PrefetchScalarGridSpec(
            num_scalar_prefetch=1,
            grid=(),
            in_specs=[vmem, pl.BlockSpec(memory_space=pltpu.HBM)]
            + ([] if total is None else [vmem]),
            out_specs=vmem,
            scratch_shapes=[
                pltpu.VMEM((count, depth, columns), weight.dtype),
                pltpu.SemaphoreType.DMA((count,)),
            ],
        ),
        out_shape=jax.ShapeDtypeStruct((rows, columns), jnp.float32),
        compiler_params=pltpu.CompilerParams(vmem_limit_bytes=12 << 20),
        name="query_step",
    )(blocks, texts, weight, *(() if total is None else (total,)))


def place_requests(ids_ref, slots_ref, counts_ref, visit):
    images = slots_ref.shape[0]
    for image in range(images):
        counts_ref[image] = 0
    for request in range(ids_ref.shape[0]):
        for which in range(ids_ref.shape[1]):
            owner = slots_ref[ids_ref[request, which]]
            taken = counts_ref[owner]
            counts_ref[owner] = taken + 1
            visit(request, which, owner * CAP + taken)


def query_last_kernel(
    ids_ref, slots_ref, total_ref, gain_ref, out_ref, normed_ref, table_ref, counts_ref
):
    width = gain_ref.shape[1]
    heads = total_ref.shape[1] // width
    words = total_ref.shape[0] // ids_ref.shape[0]
    slots = out_ref.shape[0] // words
    for slot in range(slots):
        table_ref[slot] = 0

    def visit(request, _, slot):
        table_ref[slot] = request

    place_requests(ids_ref, slots_ref, counts_ref, visit)
    for head in range(heads):
        at = pl.ds(head * width, width)
        q = total_ref[:, at]
        q = q * lax.rsqrt(jnp.mean(q * q, axis=-1, keepdims=True) + epsilon) * gain_ref[...]
        normed_ref[:, at] = (q * width ** (-0.5)).astype(jnp.bfloat16).astype(jnp.float32)
    for slot in range(0, slots, 2):
        rows = [
            normed_ref[pl.ds(pl.multiple_of(table_ref[slot + i] * words, words), words)]
            for i in range(2)
        ]
        out_ref[pl.ds(slot * words, 2 * words)] = jnp.concatenate(rows).astype(jnp.bfloat16)


def query_last(image_ids, image_slot, total, gain):
    rows, columns = total.shape
    smem = pl.BlockSpec(memory_space=pltpu.SMEM)
    vmem = pl.BlockSpec(memory_space=pltpu.VMEM)
    images = image_slot.shape[0]
    words = rows // image_ids.shape[0]
    return pl.pallas_call(
        query_last_kernel,
        in_specs=[smem, smem, vmem, vmem],
        out_specs=vmem,
        out_shape=jax.ShapeDtypeStruct((images * CAP * words, columns), jnp.bfloat16),
        scratch_shapes=[
            pltpu.VMEM((rows, columns), jnp.float32),
            pltpu.SMEM((images * CAP,), jnp.int32),
            pltpu.SMEM((images,), jnp.int32),
        ],
        compiler_params=pltpu.CompilerParams(vmem_limit_bytes=8 << 20),
        name="query_last",
    )(image_ids, image_slot, total, gain[None])


def attend_kernel(q_ref, key_ref, value_ref, out_ref):
    width = key_ref.shape[0]
    heads = q_ref.shape[1] // width
    value = value_ref[...].T
    value = jnp.concatenate([value, jnp.ones_like(value)], axis=1)
    lane = lax.broadcasted_iota(jnp.int32, (q_ref.shape[0], width), 1)
    packed = jnp.zeros(lane.shape, jnp.float32)
    for head in range(heads):
        at = pl.ds(head * width, width)
        scores = jnp.dot(q_ref[:, at], key_ref[...], preferred_element_type=jnp.float32)
        exponent = jnp.exp(scores).astype(jnp.bfloat16)
        both = jnp.dot(exponent, value, preferred_element_type=jnp.float32)
        out_ref[:, at] = both[:, :width].astype(out_ref.dtype)
        total = both[:, width:]
        coarse = total.astype(jnp.bfloat16).astype(jnp.float32)
        packed = jnp.where(lane == head, coarse, packed)
        packed = jnp.where(lane == head + heads, total - coarse, packed)
    out_ref[:, pl.ds(heads * width, width)] = packed.astype(out_ref.dtype)


def attend(queries, keys, values):
    rows, columns = queries.shape
    vmem = pl.BlockSpec(memory_space=pltpu.VMEM)
    return pl.pallas_call(
        attend_kernel,
        in_specs=[vmem] * 3,
        out_specs=vmem,
        out_shape=jax.ShapeDtypeStruct((rows, columns + keys.shape[0]), jnp.bfloat16),
        compiler_params=pltpu.CompilerParams(vmem_limit_bytes=32 << 20),
        name="attend",
    )(queries, keys, values)


def combine_kernel(ids_ref, slots_ref, back_ref, gate_ref, out_ref, table_ref, counts_ref):
    requests, images = ids_ref.shape
    words = out_ref.shape[0] // requests
    columns = out_ref.shape[1]
    width = back_ref.shape[1] - columns
    heads = columns // width

    def visit(request, which, slot):
        table_ref[request * images + which] = slot

    place_requests(ids_ref, slots_ref, counts_ref, visit)
    gate = jnp.tanh(jnp.broadcast_to(gate_ref[...], (words, width)))
    for request in range(0, requests, 2):
        results = []
        for i in range(2):
            slots = [table_ref[(request + i) * images + which] for which in range(images)]
            parts = [
                back_ref[pl.ds(pl.multiple_of(slot * words, words), words)].astype(jnp.float32)
                for slot in slots
            ]
            both = parts[0] + parts[1]
            columns_of = []
            for head in range(heads):
                low = columns + head
                total = both[:, low : low + 1] + both[:, low + heads : low + heads + 1]
                at = slice(head * width, (head + 1) * width)
                columns_of.append(gate * (both[:, at] / total))
            results.append(jnp.concatenate(columns_of, axis=1))
        out_ref[pl.ds(request * words, 2 * words)] = jnp.concatenate(results).astype(out_ref.dtype)


def combine(image_ids, image_slot, back, gate, rows):
    smem = pl.BlockSpec(memory_space=pltpu.SMEM)
    vmem = pl.BlockSpec(memory_space=pltpu.VMEM)
    width = gate.shape[1]
    return pl.pallas_call(
        combine_kernel,
        in_specs=[smem, smem, vmem, vmem],
        out_specs=vmem,
        out_shape=jax.ShapeDtypeStruct((rows, back.shape[1] - width), jnp.bfloat16),
        scratch_shapes=[
            pltpu.SMEM((image_ids.size,), jnp.int32),
            pltpu.SMEM(image_slot.shape, jnp.int32),
        ],
        compiler_params=pltpu.CompilerParams(vmem_limit_bytes=8 << 20),
        name="combine",
    )(image_ids, image_slot, back, gate)


def per_device(
    text_rows, q_weight, features, kv_weight, q_gain, k_gain, attn_gate, image_ids, image_slot
):
    rows = text_rows.shape[0]
    words = rows // image_ids.shape[0]
    images = image_slot.shape[0]
    width = q_gain.shape[0]
    columns = q_weight.shape[1]

    mine = lax.axis_index("feat").astype(jnp.int32)
    side, place = mine >> 2, mine & (RING - 1)
    q_weight = pltpu.with_memory_space_constraint(q_weight, pltpu.HBM)
    near = (place + jnp.arange(RING, dtype=jnp.int32)) & (RING - 1)

    beside = permute(text_rows, 1, 0)

    vision = features[0].T
    key_away, value_away = project((1 - side) * RING + near, kv_weight, vision, width, jnp.bfloat16)
    key_away = (key_away * KEY_SCALE).astype(jnp.float16)
    key_away, beside = lax.optimization_barrier((key_away, beside))
    key_away = permute(key_away, 1, 0)
    both_texts = jnp.stack([text_rows, beside])
    passed = {step: permute(both_texts, 0, step) for step in (1, 3, 2)}
    key_home, value_home = project(side * RING + near, kv_weight, vision, width, jnp.float32)

    sides = jnp.stack([side, 1 - side]) * RING
    queries = query_step(sides + place, both_texts, q_weight)
    value_away, key_away, key_home, value_home, queries = lax.optimization_barrier(
        (value_away, key_away, key_home, value_home, queries)
    )
    value_away = permute(value_away, 1, 0)
    for step in (1, 3, 2):
        queries = query_step(sides + ((place - step) & (RING - 1)), passed[step], q_weight, queries)
    sent = query_last(image_ids, image_slot, queries, q_gain)
    sent, key_away = lax.optimization_barrier((sent, key_away))
    arrived = lax.all_to_all(
        sent.reshape(images, CAP * words, columns), "dp", 0, 0, tiled=True
    ).reshape(images * CAP * words, columns)

    def finish(home, away, wire, scale):
        def pair(step):
            return home[step] * scale + away[step].astype(jnp.float32)

        passed = [permute(pair(step).astype(wire), 0, step) for step in (1, 3, 2)]
        return functools.reduce(lambda t, p: t + p.astype(jnp.float32), passed, pair(0))

    key = finish(key_home, key_away, jnp.float16, KEY_SCALE)
    key = (
        key
        * lax.rsqrt(jnp.mean(key * key, axis=0, keepdims=True) + epsilon * KEY_SCALE**2)
        * k_gain[:, None]
    )
    key = key.astype(jnp.bfloat16)
    value = finish(value_home, value_away, jnp.bfloat16, 1.0).astype(jnp.bfloat16)

    back = attend(arrived, key, value)
    back = lax.all_to_all(
        back.reshape(images, CAP * words, columns + width), "dp", 0, 0, tiled=True
    ).reshape(images * CAP * words, columns + width)
    gate = jnp.broadcast_to(attn_gate[None], (1, width))
    return combine(image_ids, image_slot, back, gate, rows)


def solution(mesh):
    in_specs = (
        P("dp", "feat"),
        P(None, "feat"),
        P("dp", None, "feat"),
        P("feat", None),
        P(),
        P(),
        P(),
        P("dp", None),
        P(),
    )
    return jax.shard_map(
        per_device, mesh=mesh, in_specs=in_specs, out_specs=P("dp", "feat"), check_vma=False
    )
```

time: 331 us -> 123 us (0.37)
  waiting for transfers between devices: 199 us -> 40.6 us
  matrix products: 88.4 us -> 0 us
  Pallas kernels: 0 us -> 33.2 us
  starting transfers between devices: 0.08 us -> 32.8 us
  local copies, waits for them, and re-layouts: 24.5 us -> 5.12 us
  between operations: 13.9 us -> 0.85 us
  other arithmetic: 3.55 us -> 9.59 us
    all_gather x2 -> x0, waiting for transfers between devices: 103 us -> none  [the longest x1 71.2 us: per_device(): shard_piece = lax.all_gather(keyval[None], 'dp', axis=0, tiled=True)]
    reduce_scatter x1 -> x0, waiting for transfers between devices: 95.3 us -> none  [per_device(): lax.psum_scatter(jnp.einsum('nf,fhc->hnc', vision_rows, weight_block, pre...]
    dot_general x34 -> x0, matrix products: 88.4 us -> none  [the longest x16 36.6 us: attend(): jnp.einsum('rhgd,hnd->rhgn', queries, keyval[..., :head_width], preferred...]
    pallas_call x0 -> x9, Pallas kernels: none -> 33.2 us  [the longest x4 16.3 us: query_step(): pl.pallas_call(query_step_kernel, grid_spec=pltpu.PrefetchScalarGridSpec(...]
    ppermute x0 -> x12, waiting for transfers between devices: none -> 22.6 us  [permute(): return lax.ppermute(values, 'feat', pairs)]
    all_to_all x0 -> x2, starting transfers between devices: none -> 19.1 us  [the longest x1 10.8 us: per_device(): lax.all_to_all(sent.reshape(images, CAP * words, columns), 'dp', 0, 0, ti...]
    all_to_all x0 -> x2, waiting for transfers between devices: none -> 18 us  [the longest x1 18 us: per_device(): lax.all_to_all(back.reshape(images, CAP * words, columns + width), 'dp',...]
    squeeze x16 -> x0, local copies, waits for them, and re-layouts: 17.3 us -> none  [add_one(): lax.dynamic_index_in_dim(shard_piece, position, 0, keepdims=False)]
  transfers between devices with their start and end apart: 3 -> 14, of which waited for: 3 -> 5; matrix products, arithmetic and copies ran while one was open for 4% -> 8% of each run, Pallas kernels for 0% -> 21%
where the time goes in v2:
time: 123 us; the launch traced here: 122 us
  waiting for transfers between devices  40.6 us (33%)
  Pallas kernels  33.2 us (27%)
  starting transfers between devices  32.8 us (27%)
  other arithmetic  9.59 us (8%)
  local copies, waits for them, and re-layouts  5.12 us (4%)
    ppermute x12, waiting for transfers between devices, permute(): return lax.ppermute(values, 'feat', pairs)  22.6 us
    all_to_all x1, waiting for transfers between devices, per_device(): lax.all_to_all(back.reshape(images, CAP * words, columns + width), 'dp',...  18 us
    pallas_call x4, Pallas kernels, query_step(): pl.pallas_call(query_step_kernel, grid_spec=pltpu.PrefetchScalarGridSpec(...  16.3 us
    ppermute x12, starting transfers between devices, permute(): return lax.ppermute(values, 'feat', pairs)  13.6 us
    all_to_all x1, starting transfers between devices, per_device(): lax.all_to_all(sent.reshape(images, CAP * words, columns), 'dp', 0, 0, ti...  10.8 us
    all_to_all x1, starting transfers between devices, per_device(): lax.all_to_all(back.reshape(images, CAP * words, columns + width), 'dp',...  8.37 us
    pallas_call x2, Pallas kernels, project(): pl.pallas_call(project_kernel, grid_spec=pltpu.PrefetchScalarGridSpec(num...  7.43 us
    pallas_call x1, Pallas kernels, attend(): pl.pallas_call(attend_kernel, in_specs=[vmem] * 3, out_specs=vmem, out_sh...  5.67 us
  transfers between devices with their start and end apart: 14, of which 5 were waited for; matrix products, arithmetic and copies ran while one was open for 8% of the time, Pallas kernels for 21%

profile of v2, /device:TPU:1, one launch (start us, length us, event | category | flops | bytes accessed | tf_op | source)
XLA Modules:
  0.0 122.1 jit_solution(9272081618088063537)
XLA Ops:
  0.0 2.0 %collective-permute-start = (bf16[128,1024]{1,0:T(8,128)(2,1)}, bf16[128,1024]{1,0:T(8,128)(2,1)S(1)}, u32[]{:S(2)}, u32[]{:S(2)}) collective-permute-start(bf16[128,1024]{1,0:T(8,128)(2,1)} %param.9), channel_id=1, source_target_pairs={{0,64},{16,80},{32,96},{48,112},{64,0},{80,16},{96,32},{112,48},{1... | collective-permute-start | bytes 786440 | tf_op jit(solution)/shard_map/ppermute | solution.py:22
  2.0 0.0 copy-start
  2.0 2.1 %copy-done = bf16[960,2048]{1,0:T(8,128)(2,1)S(1)} copy-done((bf16[960,2048]{1,0:T(8,128)(2,1)S(1)}, bf16[960,2048]{1,0:T(8,128)(2,1)}, u32[]{:S(2)}) %copy-start) | copy-done | bytes 3932184
  4.2 0.0 copy-start.2
  4.2 1.5 %copy-done.2 = bf16[1,1024,960]{1,2,0:T(8,128)(2,1)S(1)} copy-done((bf16[1,1024,960]{1,2,0:T(8,128)(2,1)S(1)}, bf16[1,1024,960]{1,2,0:T(8,128)(2,1)}, u32[]{:S(2)}) %copy-start.2) | copy-done | bytes 1966104
  5.7 0.0 copy-start.3
  5.7 4.2 %project.2 = (f32[4,128,1024]{2,1,0:T(8,128)S(1)}, bf16[4,128,1024]{2,1,0:T(8,128)(2,1)}) custom-call(s32[4]{0:T(128)S(1)} %get-tuple-element.43._, bf16[960,2048]{1,0:T(8,128)(2,1)S(1)} %copy-done, bf16[960,2048]{1,0:T(8,128)(2,1)S(1)} %copy-done, bf16[960,2048]{1,0:T(8,128)(2,1)S(1)} %copy-done, bf16[960,2048]{1,0:T(8,128)(2,1)S(1)} %copy-done, ...), custom_call_target="tpu_custom_call" | custom-call | tf_op jit(solution)/shard_map/project/pallas_call | solution.py:43
  9.9 1.3 %multiply_convert_fusion = f16[4,128,1024]{2,1,0:T(8,128)(2,1)} fusion(f32[4,128,1024]{2,1,0:T(8,128)S(1)} %get-tuple-element.18), kind=kLoop, calls=%fused_computation | loop fusion | flops 1048576 | bytes 3145728 | tf_op jit(solution)/shard_map/convert_element_type | solution.py:264
  11.2 0.0 collective-permute-done
  11.2 0.0 collective-permute-start.4
  11.2 0.0 copy-done.8
  11.2 0.1 pad_maximum_fusion.text_ref
  11.3 1.6 %collective-permute-start.3 = (bf16[2,128,1024]{2,1,0:T(8,128)(2,1)S(1)}, bf16[2,128,1024]{2,1,0:T(8,128)(2,1)}, u32[]{:S(2)}, u32[]{:S(2)}) collective-permute-start(bf16[2,128,1024]{2,1,0:T(8,128)(2,1)S(1)} %pad_maximum_fusion.text_ref), channel_id=1, source_target_pairs={{0,16},{16,32},{32,48},{48,0},{64,80},{80,96},{96,112},{112,64},{1... | collective-permute-start | bytes 1572872 | tf_op jit(solution)/shard_map/ppermute | solution.py:22
  12.9 1.5 %collective-permute-start.2 = (bf16[2,128,1024]{2,1,0:T(8,128)(2,1)S(1)}, bf16[2,128,1024]{2,1,0:T(8,128)(2,1)}, u32[]{:S(2)}, u32[]{:S(2)}) collective-permute-start(bf16[2,128,1024]{2,1,0:T(8,128)(2,1)S(1)} %pad_maximum_fusion.text_ref), channel_id=1, source_target_pairs={{0,48},{16,0},{32,16},{48,32},{64,112},{80,64},{96,80},{112,96},{1... | collective-permute-start | bytes 1572872 | tf_op jit(solution)/shard_map/ppermute | solution.py:22
  14.4 1.6 %collective-permute-start.1 = (bf16[2,128,1024]{2,1,0:T(8,128)(2,1)S(1)}, bf16[2,128,1024]{2,1,0:T(8,128)(2,1)}, u32[]{:S(2)}, u32[]{:S(2)}) collective-permute-start(bf16[2,128,1024]{2,1,0:T(8,128)(2,1)S(1)} %pad_maximum_fusion.text_ref), channel_id=1, source_target_pairs={{0,32},{16,48},{32,0},{48,16},{64,96},{80,112},{96,64},{112,80},{1... | collective-permute-start | bytes 1572872 | tf_op jit(solution)/shard_map/ppermute | solution.py:22
  16.0 0.0 copy-done.3
  16.0 0.0 copy-done.1
  16.0 3.2 %project.3 = (f32[4,128,1024]{2,1,0:T(8,128)S(1)}, f32[4,128,1024]{2,1,0:T(8,128)S(1)}) custom-call(s32[4]{0:T(128)S(1)} %get-tuple-element.42._, bf16[960,2048]{1,0:T(8,128)(2,1)S(1)} %copy-done.1, bf16[960,2048]{1,0:T(8,128)(2,1)S(1)} %copy-done.1, bf16[960,2048]{1,0:T(8,128)(2,1)S(1)} %copy-done.1, bf16[960,2048]{1,0:T(8,128)(2,1)S(1)} %copy-done.1, ...), custom_call_target="tpu_custom_call" | custom-call | tf_op jit(solution)/shard_map/project/pallas_call | solution.py:43
  19.2 0.0 copy-start.4
  19.2 1.3 %copy-done.4 = f32[4,128,1024]{2,1,0:T(8,128)} copy-done((f32[4,128,1024]{2,1,0:T(8,128)}, f32[4,128,1024]{2,1,0:T(8,128)S(1)}, u32[]{:S(2)}) %copy-start.4) | copy-done | bytes 2097176
  20.6 0.1 broadcast_add_fusion
  20.6 3.5 %query_step.4.refs_0_ = f32[128,1024]{1,0:T(8,128)S(1)} custom-call(s32[2]{0:T(128)S(1)} %get-tuple-element.31.blocks, bf16[2,128,1024]{2,1,0:T(8,128)(2,1)S(1)} %pad_maximum_fusion.text_ref, bf16[8192,1024]{1,0:T(8,128)(2,1)} %weight_ref.7), custom_call_target="tpu_custom_call" | custom-call | tf_op jit(solution)/shard_map/query_step/pallas_call | solution.py:85
  24.1 11.1 %collective-permute-done.4 = f16[4,128,1024]{2,1,0:T(8,128)(2,1)} collective-permute-done((f16[4,128,1024]{2,1,0:T(8,128)(2,1)}, f16[4,128,1024]{2,1,0:T(8,128)(2,1)}, u32[]{:S(2)}, u32[]{:S(2)}) %collective-permute-start.4) | collective-permute-done | bytes 1048608 | tf_op jit(solution)/shard_map/ppermute | solution.py:22
  35.3 0.0 collective-permute-start.8
  35.3 0.0 copy-done.9
  35.3 0.1 copy.11.ids_ref
  35.4 0.0 collective-permute-done.3.text_ref
  35.4 4.3 %query_step.5.refs_0_ = f32[128,1024]{1,0:T(8,128)S(1)} custom-call(s32[2]{0:T(128)S(1)} %get-tuple-element.39.blocks, bf16[2,128,1024]{2,1,0:T(8,128)(2,1)} %collective-permute-done.3.text_ref, bf16[8192,1024]{1,0:T(8,128)(2,1)} %weight_ref.7, f32[128,1024]{1,0:T(8,128)S(1)} %query_step.4.refs_0_), custom_call_target="tpu_custom_call" | custom-call | tf_op jit(solution)/shard_map/query_step/pallas_call | solution.py:85
  39.7 0.0 collective-permute-done.2.text_ref
  39.7 4.3 %query_step.6.refs_0_ = f32[128,1024]{1,0:T(8,128)S(1)} custom-call(s32[2]{0:T(128)S(1)} %get-tuple-element.40.blocks, bf16[2,128,1024]{2,1,0:T(8,128)(2,1)} %collective-permute-done.2.text_ref, bf16[8192,1024]{1,0:T(8,128)(2,1)} %weight_ref.7, f32[128,1024]{1,0:T(8,128)S(1)} %query_step.5.refs_0_), custom_call_target="tpu_custom_call" | custom-call | tf_op jit(solution)/shard_map/query_step/pallas_call | solution.py:85
  44.0 0.0 collective-permute-done.1.text_ref
  44.0 0.0 copy-start.5
  44.0 0.0 copy-start.6
  44.0 4.3 %query_step.7.total_ref = f32[128,1024]{1,0:T(8,128)S(1)} custom-call(s32[2]{0:T(128)S(1)} %get-tuple-element.41.blocks, bf16[2,128,1024]{2,1,0:T(8,128)(2,1)} %collective-permute-done.1.text_ref, bf16[8192,1024]{1,0:T(8,128)(2,1)} %weight_ref.7, f32[128,1024]{1,0:T(8,128)S(1)} %query_step.6.refs_0_), custom_call_target="tpu_custom_call" | custom-call | tf_op jit(solution)/shard_map/query_step/pallas_call | solution.py:85
  48.3 0.0 copy-done.5
  48.3 0.0 copy-done.6
  48.3 2.0 %query_last.1 = bf16[512,1024]{1,0:T(8,128)(2,1)} custom-call(s32[16,2]{1,0:T(8,128)S(1)} %copy.11.ids_ref, s32[16]{0:T(128)S(1)} %copy-done.5, f32[128,1024]{1,0:T(8,128)S(1)} %query_step.7.total_ref, f32[1,128]{1,0:T(1,128)S(1)} %bitcast.48), custom_call_target="tpu_custom_call" | custom-call | tf_op jit(solution)/shard_map/query_last/pallas_call | solution.py:149
  50.3 2.1 %fusion.5 = (f16[128,1024]{1,0:T(8,128)(2,1)}, f16[128,1024]{1,0:T(8,128)(2,1)}, f16[128,1024]{1,0:T(8,128)(2,1)}) fusion(f32[4,128,1024]{2,1,0:T(8,128)S(1)} %get-tuple-element.27, f16[4,128,1024]{2,1,0:T(8,128)(2,1)} %collective-permute-done.4), kind=kLoop, calls=%fused_computation.17 | loop fusion | flops 1572864 | bytes 3145728 | tf_op jit(solution)/shard_map/convert_element_type | solution.py:289
  52.4 1.6 %collective-permute-start.5 = (f16[128,1024]{1,0:T(8,128)(2,1)}, f16[128,1024]{1,0:T(8,128)(2,1)S(1)}, u32[]{:S(2)}, u32[]{:S(2)}) collective-permute-start(f16[128,1024]{1,0:T(8,128)(2,1)} %get-tuple-element.36), channel_id=1, source_target_pairs={{0,16},{16,32},{32,48},{48,0},{64,80},{80,96},{96,112},{112,64},{1... | collective-permute-start | bytes 786440 | tf_op jit(solution)/shard_map/ppermute | solution.py:22
  54.0 1.4 %collective-permute-start.6 = (f16[128,1024]{1,0:T(8,128)(2,1)}, f16[128,1024]{1,0:T(8,128)(2,1)}, u32[]{:S(2)}, u32[]{:S(2)}) collective-permute-start(f16[128,1024]{1,0:T(8,128)(2,1)} %get-tuple-element.38), channel_id=1, source_target_pairs={{0,48},{16,0},{32,16},{48,32},{64,112},{80,64},{96,80},{112,96},{1... | collective-permute-start | bytes 786440 | tf_op jit(solution)/shard_map/ppermute | solution.py:22
  55.4 1.7 %collective-permute-start.7 = (f16[128,1024]{1,0:T(8,128)(2,1)}, f16[128,1024]{1,0:T(8,128)(2,1)}, u32[]{:S(2)}, u32[]{:S(2)}) collective-permute-start(f16[128,1024]{1,0:T(8,128)(2,1)} %get-tuple-element.37), channel_id=1, source_target_pairs={{0,32},{16,48},{32,0},{48,16},{64,96},{80,112},{96,64},{112,80},{1... | collective-permute-start | bytes 786440 | tf_op jit(solution)/shard_map/ppermute | solution.py:22
  57.1 10.8 %all-to-all-start = ((bf16[16,32,1024]{2,1,0:T(8,128)(2,1)}), bf16[16,32,1024]{2,1,0:T(8,128)(2,1)S(1)}, u32[]{:S(2)}, u32[]{:S(2)}) async-start(bf16[16,32,1024]{2,1,0:T(8,128)(2,1)} %bitcast.8), calls=%async_computation | async-start | bytes 2097152 | tf_op jit(solution)/shard_map/all_to_all | solution.py:281
  67.8 0.0 collective-permute-done.5
  67.8 0.0 copy-start.7
  67.8 0.0 collective-permute-done.6
  67.9 0.0 collective-permute-done.7
  67.9 1.4 %multiply_reduce_fusion = f32[1024]{0:T(1024)S(1)} fusion(f16[128,1024]{1,0:T(8,128)(2,1)} %collective-permute-done.7, f16[128,1024]{1,0:T(8,128)(2,1)} %collective-permute-done.6, f16[128,1024]{1,0:T(8,128)(2,1)S(1)} %collective-permute-done.5, f16[4,128,1024]{2,1,0:T(8,128)(2,1)} %collective-permute-done.4, f32[4,128,1024]{2,1,0:T(8,128)S(1)} %get-tuple-element.27), kind=kLoop, calls=%fused_computation.13 | loop fusion | flops 1440768 | bytes 1576960 | tf_op jit(solution)/shard_map/reduce_sum | solution.py:295
  69.3 0.0 collective-permute-done.8
  69.3 1.8 %fusion.8 = (bf16[128,1024]{1,0:T(8,128)(2,1)S(1)}, bf16[128,1024]{1,0:T(8,128)(2,1)S(1)}, bf16[128,1024]{1,0:T(8,128)(2,1)S(1)}) fusion(f32[4,128,1024]{2,1,0:T(8,128)} %copy-done.4, bf16[4,128,1024]{2,1,0:T(8,128)(2,1)} %collective-permute-done.8), kind=kLoop, calls=%fused_computation.20 | loop fusion | flops 1179648 | bytes 3145728 | tf_op jit(solution)/shard_map/convert_element_type | solution.py:289
  71.2 0.9 collective-permute-start.10
  72.0 1.4 %collective-permute-start.11 = (bf16[128,1024]{1,0:T(8,128)(2,1)S(1)}, bf16[128,1024]{1,0:T(8,128)(2,1)S(1)}, u32[]{:S(2)}, u32[]{:S(2)}) collective-permute-start(bf16[128,1024]{1,0:T(8,128)(2,1)S(1)} %get-tuple-element.34), channel_id=1, source_target_pairs={{0,32},{16,48},{32,0},{48,16},{64,96},{80,112},{96,64},{112,80},{1... | collective-permute-start | bytes 786440 | tf_op jit(solution)/shard_map/ppermute | solution.py:22
  73.4 0.0 copy-done.7
  73.4 0.0 collective-permute-start.9
  73.4 0.0 copy-done.10
  73.4 1.4 %multiply_convert_fusion.1.key_ref = bf16[128,1024]{1,0:T(8,128)(2,1)S(1)} fusion(f32[128]{0:T(128)S(1)} %copy-done.10, f32[1024]{0:T(1024)S(1)} %add_rsqrt_fusion, f16[128,1024]{1,0:T(8,128)(2,1)} %collective-permute-done.7, f16[128,1024]{1,0:T(8,128)(2,1)} %collective-permute-done.6, f16[128,1024]{1,0:T(8,128)(2,1)} %copy-done.7, ...), kind=kLoop, calls=%fused_computation.12 | loop fusion | flops 1572864 | bytes 1839616 | tf_op jit(solution)/shard_map/convert_element_type | solution.py:298
  74.9 2.3 %collective-permute-done.10 = bf16[128,1024]{1,0:T(8,128)(2,1)S(1)} collective-permute-done((bf16[128,1024]{1,0:T(8,128)(2,1)S(1)}, bf16[128,1024]{1,0:T(8,128)(2,1)S(1)}, u32[]{:S(2)}, u32[]{:S(2)}) %collective-permute-start.10) | collective-permute-done | bytes 262176 | tf_op jit(solution)/shard_map/ppermute | solution.py:22
  77.2 1.9 %collective-permute-done.11 = bf16[128,1024]{1,0:T(8,128)(2,1)S(1)} collective-permute-done((bf16[128,1024]{1,0:T(8,128)(2,1)S(1)}, bf16[128,1024]{1,0:T(8,128)(2,1)S(1)}, u32[]{:S(2)}, u32[]{:S(2)}) %collective-permute-start.11) | collective-permute-done | bytes 262176 | tf_op jit(solution)/shard_map/ppermute | solution.py:22
  79.1 7.3 %collective-permute-done.9 = bf16[128,1024]{1,0:T(8,128)(2,1)S(1)} collective-permute-done((bf16[128,1024]{1,0:T(8,128)(2,1)S(1)}, bf16[128,1024]{1,0:T(8,128)(2,1)S(1)}, u32[]{:S(2)}, u32[]{:S(2)}) %collective-permute-start.9) | collective-permute-done | bytes 262176 | tf_op jit(solution)/shard_map/ppermute | solution.py:22
  86.4 1.3 %fusion.2.value_ref = bf16[128,1024]{1,0:T(8,128)(2,1)S(1)} fusion(bf16[128,1024]{1,0:T(8,128)(2,1)S(1)} %collective-permute-done.11, bf16[128,1024]{1,0:T(8,128)(2,1)S(1)} %collective-permute-done.10, bf16[128,1024]{1,0:T(8,128)(2,1)S(1)} %collective-permute-done.9, f32[4,128,1024]{2,1,0:T(8,128)} %copy-done.4, bf16[4,128,1024]{2,1,0:T(8,128)(2,1)} %collective-permute-done.8), kind=kLoop, calls=%fused_computation.5 | loop fusion | flops 1179648 | bytes 1835008 | tf_op jit(solution)/shard_map/convert_element_type | solution.py:299
  87.7 0.0 all-to-all-done
  87.7 5.7 %attend.1 = bf16[512,1152]{1,0:T(8,128)(2,1)} custom-call(bf16[512,1024]{1,0:T(8,128)(2,1)S(1)} %bitcast.47, bf16[128,1024]{1,0:T(8,128)(2,1)S(1)} %multiply_convert_fusion.1.key_ref, bf16[128,1024]{1,0:T(8,128)(2,1)S(1)} %fusion.2.value_ref), custom_call_target="tpu_custom_call" | custom-call | tf_op jit(solution)/shard_map/attend/pallas_call | solution.py:187
  93.4 8.4 %all-to-all-start.1 = ((bf16[16,32,1152]{2,1,0:T(8,128)(2,1)}), bf16[16,32,1152]{2,1,0:T(8,128)(2,1)S(1)}, u32[]{:S(2)}, u32[]{:S(2)}) async-start(bf16[16,32,1152]{2,1,0:T(8,128)(2,1)} %bitcast.18), calls=%async_computation.1 | async-start | bytes 2359296 | tf_op jit(solution)/shard_map/all_to_all | solution.py:302
  102.4 18.0 %all-to-all-done.1 = bf16[16,32,1152]{2,1,0:T(8,128)(2,1)S(1)} async-done(((bf16[16,32,1152]{2,1,0:T(8,128)(2,1)}), bf16[16,32,1152]{2,1,0:T(8,128)(2,1)S(1)}, u32[]{:S(2)}, u32[]{:S(2)}) %all-to-all-start.1) | async-done | bytes 1179680 | tf_op jit(solution)/shard_map/all_to_all | solution.py:302
  120.4 1.8 %combine.1 = bf16[128,1024]{1,0:T(8,128)(2,1)} custom-call(s32[16,2]{1,0:T(8,128)S(1)} %copy.11.ids_ref, s32[16]{0:T(128)S(1)} %copy-done.5, bf16[512,1152]{1,0:T(8,128)(2,1)S(1)} %bitcast.46, f32[1,128]{1,0:T(1,128)S(1)} %broadcast_in_dim.15.gate_ref), custom_call_target="tpu_custom_call" | custom-call | tf_op jit(solution)/shard_map/combine/pallas_call | solution.py:232
  (8 shorter events, 0.0 us)
Async XLA Ops:
  0.0 11.2 %collective-permute-start = (bf16[128,1024]{1,0:T(8,128)(2,1)}, bf16[128,1024]{1,0:T(8,128)(2,1)S(1)}, u32[]{:S(2)}, u32[]{:S(2)}) collective-permute-start(bf16[128,1024]{1,0:T(8,128)(2,1)} %param.9), channel_id=1, source_target_pairs={{0,64},{16,80},{32,96},{48,112},{64,0},{80,16},{96,32},{112,48},{1... | collective-permute-start | bytes 786440 | tf_op jit(solution)/shard_map/ppermute | solution.py:22
  2.0 2.1 %copy-start = (bf16[960,2048]{1,0:T(8,128)(2,1)S(1)}, bf16[960,2048]{1,0:T(8,128)(2,1)}, u32[]{:S(2)}) copy-start(bf16[960,2048]{1,0:T(8,128)(2,1)} %refs_7_.3) | copy-start | bytes 11796484
  4.2 1.5 %copy-start.2 = (bf16[1,1024,960]{1,2,0:T(8,128)(2,1)S(1)}, bf16[1,1024,960]{1,2,0:T(8,128)(2,1)}, u32[]{:S(2)}) copy-start(bf16[1,1024,960]{1,2,0:T(8,128)(2,1)} %param.11) | copy-start | bytes 5898244
  5.7 10.3 %copy-start.3 = (bf16[1,1024,960]{1,2,0:T(8,128)(2,1)S(1)}, bf16[1,1024,960]{1,2,0:T(8,128)(2,1)}, u32[]{:S(2)}) copy-start(bf16[1,1024,960]{1,2,0:T(8,128)(2,1)} %param.11) | copy-start | bytes 5898244
  9.9 1.3 %copy-start.8 = (bf16[128,1024]{1,0:T(8,128)(2,1)S(1)}, bf16[128,1024]{1,0:T(8,128)(2,1)}, u32[]{:S(2)}) copy-start(bf16[128,1024]{1,0:T(8,128)(2,1)} %param.9) | copy-start | bytes 786436
  9.9 6.1 %copy-start.1 = (bf16[960,2048]{1,0:T(8,128)(2,1)S(1)}, bf16[960,2048]{1,0:T(8,128)(2,1)}, u32[]{:S(2)}) copy-start(bf16[960,2048]{1,0:T(8,128)(2,1)} %refs_7_.3) | copy-start | bytes 11796484
  11.2 24.0 %collective-permute-start.4 = (f16[4,128,1024]{2,1,0:T(8,128)(2,1)}, f16[4,128,1024]{2,1,0:T(8,128)(2,1)}, u32[]{:S(2)}, u32[]{:S(2)}) collective-permute-start(f16[4,128,1024]{2,1,0:T(8,128)(2,1)} %multiply_convert_fusion), channel_id=1, source_target_pairs={{0,64},{16,80},{32,96},{48,112},{64,0},{80,16},{96,32},{112,48},{1... | collective-permute-start | bytes 3145736 | tf_op jit(solution)/shard_map/ppermute | solution.py:22
  11.3 24.1 %collective-permute-start.3 = (bf16[2,128,1024]{2,1,0:T(8,128)(2,1)S(1)}, bf16[2,128,1024]{2,1,0:T(8,128)(2,1)}, u32[]{:S(2)}, u32[]{:S(2)}) collective-permute-start(bf16[2,128,1024]{2,1,0:T(8,128)(2,1)S(1)} %pad_maximum_fusion.text_ref), channel_id=1, source_target_pairs={{0,16},{16,32},{32,48},{48,0},{64,80},{80,96},{96,112},{112,64},{1... | collective-permute-start | bytes 1572872 | tf_op jit(solution)/shard_map/ppermute | solution.py:22
  12.9 26.7 %collective-permute-start.2 = (bf16[2,128,1024]{2,1,0:T(8,128)(2,1)S(1)}, bf16[2,128,1024]{2,1,0:T(8,128)(2,1)}, u32[]{:S(2)}, u32[]{:S(2)}) collective-permute-start(bf16[2,128,1024]{2,1,0:T(8,128)(2,1)S(1)} %pad_maximum_fusion.text_ref), channel_id=1, source_target_pairs={{0,48},{16,0},{32,16},{48,32},{64,112},{80,64},{96,80},{112,96},{1... | collective-permute-start | bytes 1572872 | tf_op jit(solution)/shard_map/ppermute | solution.py:22
  14.4 29.5 %collective-permute-start.1 = (bf16[2,128,1024]{2,1,0:T(8,128)(2,1)S(1)}, bf16[2,128,1024]{2,1,0:T(8,128)(2,1)}, u32[]{:S(2)}, u32[]{:S(2)}) collective-permute-start(bf16[2,128,1024]{2,1,0:T(8,128)(2,1)S(1)} %pad_maximum_fusion.text_ref), channel_id=1, source_target_pairs={{0,32},{16,48},{32,0},{48,16},{64,96},{80,112},{96,64},{112,80},{1... | collective-permute-start | bytes 1572872 | tf_op jit(solution)/shard_map/ppermute | solution.py:22
  19.2 1.4 %copy-start.4 = (f32[4,128,1024]{2,1,0:T(8,128)}, f32[4,128,1024]{2,1,0:T(8,128)S(1)}, u32[]{:S(2)}) copy-start(f32[4,128,1024]{2,1,0:T(8,128)S(1)} %get-tuple-element.29) | copy-start | bytes 6291460
  20.6 14.6 %copy-start.9 = (s32[16,2]{0,1:T(2,128)S(1)}, s32[16,2]{0,1:T(2,128)}, u32[]{:S(2)}) copy-start(s32[16,2]{0,1:T(2,128)} %param.16) | copy-start | bytes 388
  35.3 34.0 %collective-permute-start.8 = (bf16[4,128,1024]{2,1,0:T(8,128)(2,1)}, bf16[4,128,1024]{2,1,0:T(8,128)(2,1)}, u32[]{:S(2)}, u32[]{:S(2)}) collective-permute-start(bf16[4,128,1024]{2,1,0:T(8,128)(2,1)} %get-tuple-element.30), channel_id=1, source_target_pairs={{0,64},{16,80},{32,96},{48,112},{64,0},{80,16},{96,32},{112,48},{1... | collective-permute-start | bytes 3145736 | tf_op jit(solution)/shard_map/ppermute | solution.py:22
  44.0 4.3 %copy-start.5 = (s32[16]{0:T(128)S(1)}, s32[16]{0:T(128)}, u32[]{:S(2)}) copy-start(s32[16]{0:T(128)} %slots_ref.3) | copy-start | bytes 196
  44.0 4.3 %copy-start.6 = (f32[128]{0:T(128)S(1)}, f32[128]{0:T(128)}, u32[]{:S(2)}) copy-start(f32[128]{0:T(128)} %param.13) | copy-start | bytes 1540
  52.4 15.4 %collective-permute-start.5 = (f16[128,1024]{1,0:T(8,128)(2,1)}, f16[128,1024]{1,0:T(8,128)(2,1)S(1)}, u32[]{:S(2)}, u32[]{:S(2)}) collective-permute-start(f16[128,1024]{1,0:T(8,128)(2,1)} %get-tuple-element.36), channel_id=1, source_target_pairs={{0,16},{16,32},{32,48},{48,0},{64,80},{80,96},{96,112},{112,64},{1... | collective-permute-start | bytes 786440 | tf_op jit(solution)/shard_map/ppermute | solution.py:22
  54.0 13.9 %collective-permute-start.6 = (f16[128,1024]{1,0:T(8,128)(2,1)}, f16[128,1024]{1,0:T(8,128)(2,1)}, u32[]{:S(2)}, u32[]{:S(2)}) collective-permute-start(f16[128,1024]{1,0:T(8,128)(2,1)} %get-tuple-element.38), channel_id=1, source_target_pairs={{0,48},{16,0},{32,16},{48,32},{64,112},{80,64},{96,80},{112,96},{1... | collective-permute-start | bytes 786440 | tf_op jit(solution)/shard_map/ppermute | solution.py:22
  55.4 12.5 %collective-permute-start.7 = (f16[128,1024]{1,0:T(8,128)(2,1)}, f16[128,1024]{1,0:T(8,128)(2,1)}, u32[]{:S(2)}, u32[]{:S(2)}) collective-permute-start(f16[128,1024]{1,0:T(8,128)(2,1)} %get-tuple-element.37), channel_id=1, source_target_pairs={{0,32},{16,48},{32,0},{48,16},{64,96},{80,112},{96,64},{112,80},{1... | collective-permute-start | bytes 786440 | tf_op jit(solution)/shard_map/ppermute | solution.py:22
  57.1 30.6 %all-to-all-start = ((bf16[16,32,1024]{2,1,0:T(8,128)(2,1)}), bf16[16,32,1024]{2,1,0:T(8,128)(2,1)S(1)}, u32[]{:S(2)}, u32[]{:S(2)}) async-start(bf16[16,32,1024]{2,1,0:T(8,128)(2,1)} %bitcast.8), calls=%async_computation | async-start | bytes 2097152 | tf_op jit(solution)/shard_map/all_to_all | solution.py:281
  67.8 5.6 %copy-start.10 = (f32[128]{0:T(128)S(1)}, f32[128]{0:T(128)}, u32[]{:S(2)}) copy-start(f32[128]{0:T(128)} %param.14) | copy-start | bytes 1540
  67.8 5.6 %copy-start.7 = (f16[128,1024]{1,0:T(8,128)(2,1)}, f16[128,1024]{1,0:T(8,128)(2,1)S(1)}, u32[]{:S(2)}) copy-start(f16[128,1024]{1,0:T(8,128)(2,1)S(1)} %collective-permute-done.5) | copy-start | bytes 786436
  71.2 6.1 %collective-permute-start.10 = (bf16[128,1024]{1,0:T(8,128)(2,1)S(1)}, bf16[128,1024]{1,0:T(8,128)(2,1)S(1)}, u32[]{:S(2)}, u32[]{:S(2)}) collective-permute-start(bf16[128,1024]{1,0:T(8,128)(2,1)S(1)} %get-tuple-element.35), channel_id=1, source_target_pairs={{0,48},{16,0},{32,16},{48,32},{64,112},{80,64},{96,80},{112,96},{1... | collective-permute-start | bytes 786440 | tf_op jit(solution)/shard_map/ppermute | solution.py:22
  72.0 7.0 %collective-permute-start.11 = (bf16[128,1024]{1,0:T(8,128)(2,1)S(1)}, bf16[128,1024]{1,0:T(8,128)(2,1)S(1)}, u32[]{:S(2)}, u32[]{:S(2)}) collective-permute-start(bf16[128,1024]{1,0:T(8,128)(2,1)S(1)} %get-tuple-element.34), channel_id=1, source_target_pairs={{0,32},{16,48},{32,0},{48,16},{64,96},{80,112},{96,64},{112,80},{1... | collective-permute-start | bytes 786440 | tf_op jit(solution)/shard_map/ppermute | solution.py:22
  73.4 12.9 %collective-permute-start.9 = (bf16[128,1024]{1,0:T(8,128)(2,1)S(1)}, bf16[128,1024]{1,0:T(8,128)(2,1)S(1)}, u32[]{:S(2)}, u32[]{:S(2)}) collective-permute-start(bf16[128,1024]{1,0:T(8,128)(2,1)S(1)} %get-tuple-element.33), channel_id=1, source_target_pairs={{0,16},{16,32},{32,48},{48,0},{64,80},{80,96},{96,112},{112,64},{1... | collective-permute-start | bytes 786440 | tf_op jit(solution)/shard_map/ppermute | solution.py:22
  93.4 27.0 %all-to-all-start.1 = ((bf16[16,32,1152]{2,1,0:T(8,128)(2,1)}), bf16[16,32,1152]{2,1,0:T(8,128)(2,1)S(1)}, u32[]{:S(2)}, u32[]{:S(2)}) async-start(bf16[16,32,1152]{2,1,0:T(8,128)(2,1)} %bitcast.18), calls=%async_computation.1 | async-start | bytes 2359296 | tf_op jit(solution)/shard_map/all_to_all | solution.py:302

commit v3 on v2

--- a/solution.py
+++ b/solution.py
@@ -11,6 +11,7 @@
 CAP = 4
 RING = 4
 KEY_SCALE = 64.0
+COST = pl.CostEstimate(flops=0, transcendentals=0, bytes_accessed=0)
 
 
 def permute(values, across, along):
@@ -22,83 +23,105 @@
     return lax.ppermute(values, "feat", pairs)
 
 
-def project_kernel(_, *refs):
-    weights, (vision_ref, key_ref, value_ref) = refs[: 2 * RING], refs[2 * RING :]
-    for part, out_ref in enumerate((key_ref, value_ref)):
-        weight = jnp.concatenate([w[...] for w in weights[part::2]], axis=1)
+def project_kernel(_, *refs, outs):
+    vision_ref, out_refs = refs[-1 - outs], refs[-outs:]
+    for out_ref in out_refs:
+        count = out_ref.shape[0]
+        weight = jnp.concatenate([w[...] for w in refs[:count]], axis=1)
+        refs = refs[count:]
         product = lax.dot_general(
             weight, vision_ref[...], (((0,), (0,)), ((), ())), preferred_element_type=jnp.float32
         )
         out_ref[...] = product.reshape(out_ref.shape).astype(out_ref.dtype)
 
 
-def project(heads, kv_weight, vision, width, value_type):
+def device_at(mine, across, along):
+    return ((mine[0] // RING) ^ across) * RING + ((mine[0] + along) & (RING - 1))
+
+
+def project(mine, kv_weight, vision, width, outs, shape=jax.ShapeDtypeStruct):
     depth, tokens = vision.shape
-    specs = [
-        pl.BlockSpec((depth, width), functools.partial(lambda j, part, g, h: (0, 2 * h[j] + part), j, part))
-        for j in range(RING)
-        for part in range(2)
-    ]
-    out = pl.BlockSpec((RING, width, tokens), lambda g, h: (0, 0, 0))
-    return pl.pallas_call(
-        project_kernel,
+
+    def block(across, part, along, _, mine):
+        return 0, 2 * device_at(mine, across, along) + part
+
+    return pl.pallas_call(
+        functools.partial(project_kernel, outs=len(outs)),
         grid_spec=pltpu.PrefetchScalarGridSpec(
             num_scalar_prefetch=1,
             grid=(1,),
-            in_specs=specs + [pl.BlockSpec((depth, tokens), lambda g, h: (0, 0))],
-            out_specs=[out, out],
+            in_specs=[
+                pl.BlockSpec((depth, width), functools.partial(block, across, part, along))
+                for across, part, _ in outs
+                for along in range(RING)
+            ]
+            + [pl.BlockSpec((depth, tokens), lambda g, m: (0, 0))],
+            out_specs=[pl.BlockSpec((RING, width, tokens), lambda g, m: (0, 0, 0))] * len(outs),
         ),
-        out_shape=[
-            jax.ShapeDtypeStruct((RING, width, tokens), jnp.float32),
-            jax.ShapeDtypeStruct((RING, width, tokens), value_type),
-        ],
+        out_shape=[shape((RING, width, tokens), kind) for _, _, kind in outs],
         compiler_params=pltpu.CompilerParams(vmem_limit_bytes=24 << 20),
         name="project",
-    )(heads, *([kv_weight] * (2 * RING)), vision)
-
-
-def query_step_kernel(blocks, text_ref, weight_ref, *refs):
-    total_ref, block_ref, sems = refs[-3:]
-    count, _, depth = text_ref.shape
+        cost_estimate=COST,
+    )(mine, *([kv_weight] * (RING * len(outs))), vision)
+
+
+def add_products(mine, places, text_refs, weight_ref, block_ref, sems, total):
+    pieces = [(ref, i) for ref in text_refs for i in range(ref.shape[0])]
+    blocks = [device_at(mine, across, along) for across, along in places]
+    depth = block_ref.shape[1]
     copies = [
         pltpu.make_async_copy(
-            weight_ref.at[pl.ds(pl.multiple_of(blocks[i] * depth, depth), depth)],
-            block_ref.at[i],
-            sems.at[i],
+            weight_ref.at[pl.ds(pl.multiple_of(blocks[n] * depth, depth), depth)],
+            block_ref.at[n],
+            sems.at[n],
         )
-        for i in range(count)
+        for n in range(len(pieces))
     ]
     for copy in copies:
         copy.start()
-    total = refs[0][...] if len(refs) == 4 else None
-    for i, copy in enumerate(copies):
-        copy.wait()
-        product = jnp.dot(text_ref[i], block_ref[i], preferred_element_type=jnp.float32)
+    for n, (ref, i) in enumerate(pieces):
+        copies[n].wait()
+        product = jnp.dot(ref[i], block_ref[n], preferred_element_type=jnp.float32)
         total = product if total is None else total + product
-    total_ref[...] = total
-
-
-def query_step(blocks, texts, weight, total=None):
-    count, rows, depth = texts.shape
-    columns = weight.shape[1]
+    return total
+
+
+def query_step_kernel(mine, *refs, places, first, count):
+    texts, weight_ref = refs[:count], refs[count]
+    total_ref, block_ref, sems = refs[-3:]
+    total = None if first else refs[count + 1][...]
+    total_ref[...] = add_products(mine, places, texts, weight_ref, block_ref, sems, total)
+
+
+def step_scratch(texts, weight):
+    pieces = sum(text.shape[0] for text in texts)
+    return [
+        pltpu.VMEM((pieces, texts[0].shape[2], weight.shape[1]), weight.dtype),
+        pltpu.SemaphoreType.DMA((pieces,)),
+    ]
+
+
+def query_step(mine, places, texts, weight, total=None):
     vmem = pl.BlockSpec(memory_space=pltpu.VMEM)
-    return pl.pallas_call(
-        query_step_kernel,
+    totals = () if total is None else (total,)
+    return pl.pallas_call(
+        functools.partial(
+            query_step_kernel, places=places, first=total is None, count=len(texts)
+        ),
         grid_spec=pltpu.PrefetchScalarGridSpec(
             num_scalar_prefetch=1,
             grid=(),
-            in_specs=[vmem, pl.BlockSpec(memory_space=pltpu.HBM)]
-            + ([] if total is None else [vmem]),
+            in_specs=[vmem] * len(texts)
+            + [pl.BlockSpec(memory_space=pltpu.HBM)]
+            + [vmem] * len(totals),
             out_specs=vmem,
-            scratch_shapes=[
-                pltpu.VMEM((count, depth, columns), weight.dtype),
-                pltpu.SemaphoreType.DMA((count,)),
-            ],
+            scratch_shapes=step_scratch(texts, weight),
         ),
-        out_shape=jax.ShapeDtypeStruct((rows, columns), jnp.float32),
-        compiler_params=pltpu.CompilerParams(vmem_limit_bytes=12 << 20),
+        out_shape=jax.ShapeDtypeStruct((texts[0].shape[1], weight.shape[1]), jnp.float32),
+        compiler_params=pltpu.CompilerParams(vmem_limit_bytes=16 << 20),
         name="query_step",
-    )(blocks, texts, weight, *(() if total is None else (total,)))
+        cost_estimate=COST,
+    )(mine, *texts, weight, *totals)
 
 
 def place_requests(ids_ref, slots_ref, counts_ref, visit):
@@ -113,13 +136,14 @@
             visit(request, which, owner * CAP + taken)
 
 
-def query_last_kernel(
-    ids_ref, slots_ref, total_ref, gain_ref, out_ref, normed_ref, table_ref, counts_ref
-):
+def query_last_kernel(mine, ids_ref, slots_ref, *refs, places, count):
+    texts, (weight_ref, total_ref, gain_ref, out_ref) = refs[:count], refs[count : count + 4]
+    normed_ref, table_ref, counts_ref, block_ref, sems = refs[count + 4 :]
     width = gain_ref.shape[1]
     heads = total_ref.shape[1] // width
     words = total_ref.shape[0] // ids_ref.shape[0]
     slots = out_ref.shape[0] // words
+    total = add_products(mine, places, texts, weight_ref, block_ref, sems, total_ref[...])
     for slot in range(slots):
         table_ref[slot] = 0
 
@@ -128,8 +152,8 @@
 
     place_requests(ids_ref, slots_ref, counts_ref, visit)
     for head in range(heads):
-        at = pl.ds(head * width, width)
-        q = total_ref[:, at]
+        at = slice(head * width, (head + 1) * width)
+        q = total[:, at]
         q = q * lax.rsqrt(jnp.mean(q * q, axis=-1, keepdims=True) + epsilon) * gain_ref[...]
         normed_ref[:, at] = (q * width ** (-0.5)).astype(jnp.bfloat16).astype(jnp.float32)
     for slot in range(0, slots, 2):
@@ -140,25 +164,32 @@
         out_ref[pl.ds(slot * words, 2 * words)] = jnp.concatenate(rows).astype(jnp.bfloat16)
 
 
-def query_last(image_ids, image_slot, total, gain):
+def query_last(mine, places, image_ids, image_slot, texts, weight, total, gain):
     rows, columns = total.shape
     smem = pl.BlockSpec(memory_space=pltpu.SMEM)
     vmem = pl.BlockSpec(memory_space=pltpu.VMEM)
     images = image_slot.shape[0]
     words = rows // image_ids.shape[0]
     return pl.pallas_call(
-        query_last_kernel,
-        in_specs=[smem, smem, vmem, vmem],
-        out_specs=vmem,
+        functools.partial(query_last_kernel, places=places, count=len(texts)),
+        grid_spec=pltpu.PrefetchScalarGridSpec(
+            num_scalar_prefetch=1,
+            grid=(),
+            in_specs=[smem, smem]
+            + [vmem] * len(texts)
+            + [pl.BlockSpec(memory_space=pltpu.HBM), vmem, vmem],
+            out_specs=vmem,
+            scratch_shapes=[
+                pltpu.VMEM((rows, columns), jnp.float32),
+                pltpu.SMEM((images * CAP,), jnp.int32),
+                pltpu.SMEM((images,), jnp.int32),
+            ]
+            + step_scratch(texts, weight),
+        ),
         out_shape=jax.ShapeDtypeStruct((images * CAP * words, columns), jnp.bfloat16),
-        scratch_shapes=[
-            pltpu.VMEM((rows, columns), jnp.float32),
-            pltpu.SMEM((images * CAP,), jnp.int32),
-            pltpu.SMEM((images,), jnp.int32),
-        ],
-        compiler_params=pltpu.CompilerParams(vmem_limit_bytes=8 << 20),
+        compiler_params=pltpu.CompilerParams(vmem_limit_bytes=16 << 20),
         name="query_last",
-    )(image_ids, image_slot, total, gain[None])
+    )(mine, image_ids, image_slot, *texts, weight, total, gain[None])
 
 
 def attend_kernel(q_ref, key_ref, value_ref, out_ref):
@@ -252,31 +283,41 @@
     width = q_gain.shape[0]
     columns = q_weight.shape[1]
 
-    mine = lax.axis_index("feat").astype(jnp.int32)
-    side, place = mine >> 2, mine & (RING - 1)
+    mine = lax.axis_index("feat").astype(jnp.int32).reshape(1)
+    kv_weight = pltpu.with_memory_space_constraint(kv_weight, pltpu.HBM)
     q_weight = pltpu.with_memory_space_constraint(q_weight, pltpu.HBM)
-    near = (place + jnp.arange(RING, dtype=jnp.int32)) & (RING - 1)
 
     beside = permute(text_rows, 1, 0)
 
     vision = features[0].T
-    key_away, value_away = project((1 - side) * RING + near, kv_weight, vision, width, jnp.bfloat16)
+    (key_away,) = project(mine, kv_weight, vision, width, [(1, 0, jnp.float32)])
     key_away = (key_away * KEY_SCALE).astype(jnp.float16)
     key_away, beside = lax.optimization_barrier((key_away, beside))
     key_away = permute(key_away, 1, 0)
+
     both_texts = jnp.stack([text_rows, beside])
-    passed = {step: permute(both_texts, 0, step) for step in (1, 3, 2)}
-    key_home, value_home = project(side * RING + near, kv_weight, vision, width, jnp.float32)
-
-    sides = jnp.stack([side, 1 - side]) * RING
-    queries = query_step(sides + place, both_texts, q_weight)
-    value_away, key_away, key_home, value_home, queries = lax.optimization_barrier(
-        (value_away, key_away, key_home, value_home, queries)
-    )
+    before = permute(both_texts, 0, 1)
+    behind = permute(both_texts, 0, RING - 1)
+
+    queries = query_step(mine, [(0, 0), (1, 0)], [both_texts], q_weight)
+    mine, queries = lax.optimization_barrier((mine, queries))
+    value_away, key_home, value_home = project(
+        mine,
+        kv_weight,
+        vision,
+        width,
+        [(1, 1, jnp.bfloat16), (0, 0, jnp.float32), (0, 1, jnp.float32)],
+        pltpu.HBM,
+    )
+    before, behind, value_away = lax.optimization_barrier((before, behind, value_away))
+    around = [permute(before[:1], 0, 1), permute(behind[1:], 0, RING - 1)]
     value_away = permute(value_away, 1, 0)
-    for step in (1, 3, 2):
-        queries = query_step(sides + ((place - step) & (RING - 1)), passed[step], q_weight, queries)
-    sent = query_last(image_ids, image_slot, queries, q_gain)
+    places = [(0, -1), (1, -1), (0, 1), (1, 1)]
+    queries = query_step(mine, places, [before, behind], q_weight, queries)
+    key_away, queries = lax.optimization_barrier((key_away, queries))
+    sent = query_last(
+        mine, [(0, 2), (1, 2)], image_ids, image_slot, around, q_weight, queries, q_gain
+    )
     sent, key_away = lax.optimization_barrier((sent, key_away))
     arrived = lax.all_to_all(
         sent.reshape(images, CAP * words, columns), "dp", 0, 0, tiled=True

time: 123 us -> 110 us (0.89)
  waiting for transfers between devices: 40.6 us -> 30.8 us
  starting transfers between devices: 32.8 us -> 38.1 us
  Pallas kernels: 33.2 us -> 29 us
  local copies, waits for them, and re-layouts: 5.12 us -> 2.41 us
    ppermute x12 -> x13, waiting for transfers between devices: 22.6 us -> 12.8 us  [permute(): return lax.ppermute(values, 'feat', pairs)]
    pallas_call x7 -> x5, Pallas kernels: 25.8 us -> 21.5 us  [the longest x2 9.7 us: project(): pl.pallas_call(functools.partial(project_kernel, outs=len(outs)), grid_sp...]
    unnamed x23 -> x21, local copies, waits for them, and re-layouts: 5.12 us -> 1.67 us
    ppermute x12 -> x13, starting transfers between devices: 13.6 us -> 16.3 us  [permute(): return lax.ppermute(values, 'feat', pairs)]
    all_to_all x1, starting transfers between devices: 10.8 us -> 13.2 us  [per_device(): lax.all_to_all(sent.reshape(images, CAP * words, columns), 'dp', 0, 0, ti...]
  transfers between devices with their start and end apart: 14 -> 15, of which waited for: 5 -> 5; matrix products, arithmetic and copies ran while one was open for 8% -> 8% of each run, Pallas kernels for 21% -> 20%
where the time goes in v3:
time: 110 us
  starting transfers between devices  38.1 us (35%)
  waiting for transfers between devices  30.8 us (28%)
  Pallas kernels  29 us (26%)
  other arithmetic  8.38 us (8%)
  local copies, waits for them, and re-layouts  2.41 us (2%)
    all_to_all x1, waiting for transfers between devices, per_device(): lax.all_to_all(back.reshape(images, CAP * words, columns + width), 'dp',...  18 us
    ppermute x13, starting transfers between devices, permute(): return lax.ppermute(values, 'feat', pairs)  16.3 us
    all_to_all x1, starting transfers between devices, per_device(): lax.all_to_all(sent.reshape(images, CAP * words, columns), 'dp', 0, 0, ti...  13.2 us
    ppermute x13, waiting for transfers between devices, permute(): return lax.ppermute(values, 'feat', pairs)  12.8 us
    pallas_call x2, Pallas kernels, project(): pl.pallas_call(functools.partial(project_kernel, outs=len(outs)), grid_sp...  9.7 us
    all_to_all x1, starting transfers between devices, per_device(): lax.all_to_all(back.reshape(images, CAP * words, columns + width), 'dp',...  8.62 us
    pallas_call x2, Pallas kernels, query_step(): pl.pallas_call(functools.partial(query_step_kernel, places=places, first=...  6.95 us
    pallas_call x1, Pallas kernels, attend(): pl.pallas_call(attend_kernel, in_specs=[vmem] * 3, out_specs=vmem, out_sh...  5.71 us
  transfers between devices with their start and end apart: 15, of which 5 were waited for; matrix products, arithmetic and copies ran while one was open for 8% of the time, Pallas kernels for 20%

profile of v3, /device:TPU:1, one launch (start us, length us, event | category | flops | bytes accessed | tf_op | source)
XLA Modules:
  0.0 109.6 jit_solution(514047416832630234)
XLA Ops:
  0.0 2.0 %collective-permute-start = (bf16[128,1024]{1,0:T(8,128)(2,1)}, bf16[128,1024]{1,0:T(8,128)(2,1)S(1)}, u32[]{:S(2)}, u32[]{:S(2)}) collective-permute-start(bf16[128,1024]{1,0:T(8,128)(2,1)} %param.9), channel_id=1, source_target_pairs={{0,64},{16,80},{32,96},{48,112},{64,0},{80,16},{96,32},{112,48},{1... | collective-permute-start | bytes 786440 | tf_op jit(solution)/shard_map/ppermute | solution.py:23
  2.0 0.0 copy-start
  2.0 1.5 %copy-done = bf16[1,1024,960]{1,2,0:T(8,128)(2,1)S(1)} copy-done((bf16[1,1024,960]{1,2,0:T(8,128)(2,1)S(1)}, bf16[1,1024,960]{1,2,0:T(8,128)(2,1)}, u32[]{:S(2)}) %copy-start) | copy-done | bytes 1966104
  3.6 2.6 %project.2 = f32[4,128,1024]{2,1,0:T(8,128)S(1)} custom-call(s32[1]{0:T(128)} %bitcast._.mine, bf16[960,2048]{1,0:T(8,128)(2,1)} %refs_11_.1, bf16[960,2048]{1,0:T(8,128)(2,1)} %refs_11_.1, bf16[960,2048]{1,0:T(8,128)(2,1)} %refs_11_.1, bf16[960,2048]{1,0:T(8,128)(2,1)} %refs_11_.1, bf16[960,1024]{1,0:T(8,128)(2,1)S(1)} %bitcast.43), custom_call_target="tpu_custom_call" | custom-call | tf_op jit(solution)/shard_map/project/pallas_call | solution.py:48
  6.2 0.0 copy-start.7
  6.2 1.2 %multiply_convert_fusion = f16[4,128,1024]{2,1,0:T(8,128)(2,1)} fusion(f32[4,128,1024]{2,1,0:T(8,128)S(1)} %project.2), kind=kLoop, calls=%fused_computation | loop fusion | flops 1048576 | bytes 3145728 | tf_op jit(solution)/shard_map/convert_element_type | solution.py:294
  7.5 0.3 collective-permute-done
  7.8 1.7 %collective-permute-start.5 = (f16[4,128,1024]{2,1,0:T(8,128)(2,1)}, f16[4,128,1024]{2,1,0:T(8,128)(2,1)S(1)}, u32[]{:S(2)}, u32[]{:S(2)}) collective-permute-start(f16[4,128,1024]{2,1,0:T(8,128)(2,1)} %multiply_convert_fusion), channel_id=1, source_target_pairs={{0,64},{16,80},{32,96},{48,112},{64,0},{80,16},{96,32},{112,48},{1... | collective-permute-start | bytes 3145736 | tf_op jit(solution)/shard_map/ppermute | solution.py:23
  9.4 0.0 copy-done.7
  9.4 0.1 pad_maximum_fusion.refs_0_
  9.5 2.8 %collective-permute-start.2 = (bf16[2,128,1024]{2,1,0:T(8,128)(2,1)S(1)}, bf16[2,128,1024]{2,1,0:T(8,128)(2,1)S(1)}, u32[]{:S(2)}, u32[]{:S(2)}) collective-permute-start(bf16[2,128,1024]{2,1,0:T(8,128)(2,1)S(1)} %pad_maximum_fusion.refs_0_), channel_id=1, source_target_pairs={{0,48},{16,0},{32,16},{48,32},{64,112},{80,64},{96,80},{112,96},{1... | collective-permute-start | bytes 1572872 | tf_op jit(solution)/shard_map/ppermute | solution.py:23
  12.3 0.0 collective-permute-start.1
  12.3 3.0 %query_step.2.refs_3_ = f32[128,1024]{1,0:T(8,128)S(1)} custom-call(s32[1]{0:T(128)} %bitcast._.mine, bf16[2,128,1024]{2,1,0:T(8,128)(2,1)S(1)} %pad_maximum_fusion.refs_0_, bf16[8192,1024]{1,0:T(8,128)(2,1)} %refs_2_.7), custom_call_target="tpu_custom_call" | custom-call | tf_op jit(solution)/shard_map/query_step/pallas_call | solution.py:107
  15.3 0.0 copy-start.8
  15.3 7.1 %project.3 = (bf16[4,128,1024]{2,1,0:T(8,128)(2,1)}, f32[4,128,1024]{2,1,0:T(8,128)}, f32[4,128,1024]{2,1,0:T(8,128)}) custom-call(s32[1]{0:T(128)} %bitcast._.mine, bf16[960,2048]{1,0:T(8,128)(2,1)} %refs_11_.1, bf16[960,2048]{1,0:T(8,128)(2,1)} %refs_11_.1, bf16[960,2048]{1,0:T(8,128)(2,1)} %refs_11_.1, bf16[960,2048]{1,0:T(8,128)(2,1)} %refs_11_.1, ...), custom_call_target="tpu_custom_call" | custom-call | tf_op jit(solution)/shard_map/project/pallas_call | solution.py:48
  22.4 0.0 collective-permute-done.2.refs_1_
  22.4 2.4 %collective-permute-done.1.refs_0_ = bf16[2,128,1024]{2,1,0:T(8,128)(2,1)S(1)} collective-permute-done((bf16[2,128,1024]{2,1,0:T(8,128)(2,1)S(1)}, bf16[2,128,1024]{2,1,0:T(8,128)(2,1)S(1)}, u32[]{:S(2)}, u32[]{:S(2)}) %collective-permute-start.1) | collective-permute-done | bytes 524320 | tf_op jit(solution)/shard_map/ppermute | solution.py:23
  24.8 0.7 slice.54
  25.6 0.0 collective-permute-start.3
  25.6 2.7 %collective-permute-start.4 = (bf16[1,128,1024]{2,1,0:T(8,128)(2,1)S(1)}, bf16[1,128,1024]{2,1,0:T(8,128)(2,1)S(1)}, u32[]{:S(2)}, u32[]{:S(2)}) collective-permute-start(bf16[1,128,1024]{2,1,0:T(8,128)(2,1)S(1)} %slice.55), channel_id=1, source_target_pairs={{0,48},{16,0},{32,16},{48,32},{64,112},{80,64},{96,80},{112,96},{1... | collective-permute-start | bytes 786440 | tf_op jit(solution)/shard_map/ppermute | solution.py:23
  28.2 0.3 collective-permute-start.9
  28.5 0.0 copy-done.8
  28.5 0.1 copy.11.ids_ref
  28.6 0.0 copy-start.1
  28.6 4.0 %query_step.3.refs_3_ = f32[128,1024]{1,0:T(8,128)S(1)} custom-call(s32[1]{0:T(128)} %bitcast._.mine, bf16[2,128,1024]{2,1,0:T(8,128)(2,1)S(1)} %collective-permute-done.1.refs_0_, bf16[2,128,1024]{2,1,0:T(8,128)(2,1)S(1)} %collective-permute-done.2.refs_1_, bf16[8192,1024]{1,0:T(8,128)(2,1)} %refs_2_.7, f32[128,1024]{1,0:T(8,128)S(1)} %query_step.2.refs_3_), custom_call_target="tpu_custom_call" | custom-call | tf_op jit(solution)/shard_map/query_step/pallas_call | solution.py:107
  32.6 0.0 collective-permute-done.5
  32.6 0.0 copy-start.5
  32.6 0.0 collective-permute-done.3.refs_0_
  32.6 0.0 collective-permute-done.4.refs_1_
  32.6 0.0 copy-done.1
  32.6 0.0 copy-done.2
  32.6 0.0 copy-start.3
  32.6 4.9 %query_last.1 = bf16[512,1024]{1,0:T(8,128)(2,1)} custom-call(s32[1]{0:T(128)} %bitcast._.mine, s32[16,2]{1,0:T(8,128)S(1)} %copy.11.ids_ref, s32[16]{0:T(128)S(1)} %copy-done.1, bf16[1,128,1024]{2,1,0:T(8,128)(2,1)S(1)} %collective-permute-done.3.refs_0_, bf16[1,128,1024]{2,1,0:T(8,128)(2,1)S(1)} %collective-permute-done.4.refs_1_, ...), custom_call_target="tpu_custom_call" | custom-call | tf_op jit(solution)/shard_map/query_last/pallas_call | solution.py:173
  37.5 0.0 copy-done.5
  37.5 0.0 copy-done.3
  37.5 0.0 copy-start.4
  37.6 1.0 fusion.5
  38.6 0.3 collective-permute-start.6
  38.9 2.7 %collective-permute-start.8 = (f16[128,1024]{1,0:T(8,128)(2,1)}, f16[128,1024]{1,0:T(8,128)(2,1)}, u32[]{:S(2)}, u32[]{:S(2)}) collective-permute-start(f16[128,1024]{1,0:T(8,128)(2,1)} %get-tuple-element.37), channel_id=1, source_target_pairs={{0,32},{16,48},{32,0},{48,16},{64,96},{80,112},{96,64},{112,80},{1... | collective-permute-start | bytes 786440 | tf_op jit(solution)/shard_map/ppermute | solution.py:23
  41.5 1.0 collective-permute-start.7
  42.5 13.2 %all-to-all-start = ((bf16[16,32,1024]{2,1,0:T(8,128)(2,1)}), bf16[16,32,1024]{2,1,0:T(8,128)(2,1)S(1)}, u32[]{:S(2)}, u32[]{:S(2)}) async-start(bf16[16,32,1024]{2,1,0:T(8,128)(2,1)} %bitcast.7), calls=%async_computation | async-start | bytes 2097152 | tf_op jit(solution)/shard_map/all_to_all | solution.py:322
  55.7 0.0 collective-permute-done.6
  55.7 0.0 copy-start.6
  55.7 0.0 collective-permute-done.8
  55.7 0.0 collective-permute-done.7
  55.8 0.0 copy-done.4
  55.8 1.4 %multiply_reduce_fusion = f32[1024]{0:T(1024)S(1)} fusion(f16[128,1024]{1,0:T(8,128)(2,1)} %collective-permute-done.8, f16[128,1024]{1,0:T(8,128)(2,1)} %collective-permute-done.7, f16[128,1024]{1,0:T(8,128)(2,1)S(1)} %collective-permute-done.6, f16[4,128,1024]{2,1,0:T(8,128)(2,1)} %copy-done.5, f32[4,128,1024]{2,1,0:T(8,128)S(1)} %copy-done.4), kind=kLoop, calls=%fused_computation.13 | loop fusion | flops 1440768 | bytes 1576960 | tf_op jit(solution)/shard_map/reduce_sum | solution.py:336
  57.2 0.0 collective-permute-done.9
  57.2 1.8 %fusion.8 = (bf16[128,1024]{1,0:T(8,128)(2,1)S(1)}, bf16[128,1024]{1,0:T(8,128)(2,1)S(1)}, bf16[128,1024]{1,0:T(8,128)(2,1)S(1)}) fusion(f32[4,128,1024]{2,1,0:T(8,128)} %get-tuple-element.31, bf16[4,128,1024]{2,1,0:T(8,128)(2,1)} %collective-permute-done.9), kind=kLoop, calls=%fused_computation.20 | loop fusion | flops 1179648 | bytes 3145728 | tf_op jit(solution)/shard_map/convert_element_type | solution.py:330
  59.1 0.0 copy-done.6
  59.1 0.5 collective-permute-start.10
  59.5 0.5 collective-permute-start.12
  60.1 2.0 %collective-permute-start.11 = (bf16[128,1024]{1,0:T(8,128)(2,1)S(1)}, bf16[128,1024]{1,0:T(8,128)(2,1)S(1)}, u32[]{:S(2)}, u32[]{:S(2)}) collective-permute-start(bf16[128,1024]{1,0:T(8,128)(2,1)S(1)} %get-tuple-element.35), channel_id=1, source_target_pairs={{0,48},{16,0},{32,16},{48,32},{64,112},{80,64},{96,80},{112,96},{1... | collective-permute-start | bytes 786440 | tf_op jit(solution)/shard_map/ppermute | solution.py:23
  62.0 0.0 copy-done.9
  62.0 1.5 %multiply_convert_fusion.1.key_ref = bf16[128,1024]{1,0:T(8,128)(2,1)S(1)} fusion(f32[128]{0:T(128)S(1)} %copy-done.9, f32[1024]{0:T(1024)S(1)} %add_rsqrt_fusion, f16[128,1024]{1,0:T(8,128)(2,1)} %collective-permute-done.8, f16[128,1024]{1,0:T(8,128)(2,1)} %collective-permute-done.7, f16[128,1024]{1,0:T(8,128)(2,1)} %copy-done.6, ...), kind=kLoop, calls=%fused_computation.12 | loop fusion | flops 1572864 | bytes 1839616 | tf_op jit(solution)/shard_map/convert_element_type | solution.py:339
  63.5 9.7 %collective-permute-done.10 = bf16[128,1024]{1,0:T(8,128)(2,1)S(1)} collective-permute-done((bf16[128,1024]{1,0:T(8,128)(2,1)S(1)}, bf16[128,1024]{1,0:T(8,128)(2,1)S(1)}, u32[]{:S(2)}, u32[]{:S(2)}) %collective-permute-start.10) | collective-permute-done | bytes 262176 | tf_op jit(solution)/shard_map/ppermute | solution.py:23
  73.2 0.0 collective-permute-done.12
  73.2 0.4 collective-permute-done.11
  73.6 1.3 %fusion.2.value_ref = bf16[128,1024]{1,0:T(8,128)(2,1)S(1)} fusion(bf16[128,1024]{1,0:T(8,128)(2,1)S(1)} %collective-permute-done.12, bf16[128,1024]{1,0:T(8,128)(2,1)S(1)} %collective-permute-done.11, bf16[128,1024]{1,0:T(8,128)(2,1)S(1)} %collective-permute-done.10, f32[4,128,1024]{2,1,0:T(8,128)} %get-tuple-element.31, ...), kind=kLoop, calls=%fused_computation.5 | loop fusion | flops 1179648 | bytes 1835008 | tf_op jit(solution)/shard_map/convert_element_type | solution.py:340
  74.9 0.0 all-to-all-done
  74.9 5.7 %attend.1 = bf16[512,1152]{1,0:T(8,128)(2,1)} custom-call(bf16[512,1024]{1,0:T(8,128)(2,1)S(1)} %bitcast.46, bf16[128,1024]{1,0:T(8,128)(2,1)S(1)} %multiply_convert_fusion.1.key_ref, bf16[128,1024]{1,0:T(8,128)(2,1)S(1)} %fusion.2.value_ref), custom_call_target="tpu_custom_call" | custom-call | tf_op jit(solution)/shard_map/attend/pallas_call | solution.py:218
  80.6 8.6 %all-to-all-start.1 = ((bf16[16,32,1152]{2,1,0:T(8,128)(2,1)}), bf16[16,32,1152]{2,1,0:T(8,128)(2,1)S(1)}, u32[]{:S(2)}, u32[]{:S(2)}) async-start(bf16[16,32,1152]{2,1,0:T(8,128)(2,1)} %bitcast.17), calls=%async_computation.1 | async-start | bytes 2359296 | tf_op jit(solution)/shard_map/all_to_all | solution.py:343
  89.9 18.0 %all-to-all-done.1 = bf16[16,32,1152]{2,1,0:T(8,128)(2,1)S(1)} async-done(((bf16[16,32,1152]{2,1,0:T(8,128)(2,1)}), bf16[16,32,1152]{2,1,0:T(8,128)(2,1)S(1)}, u32[]{:S(2)}, u32[]{:S(2)}) %all-to-all-start.1) | async-done | bytes 1179680 | tf_op jit(solution)/shard_map/all_to_all | solution.py:343
  107.9 1.8 %combine.1 = bf16[128,1024]{1,0:T(8,128)(2,1)} custom-call(s32[16,2]{1,0:T(8,128)S(1)} %copy.11.ids_ref, s32[16]{0:T(128)S(1)} %copy-done.1, bf16[512,1152]{1,0:T(8,128)(2,1)S(1)} %bitcast.45, f32[1,128]{1,0:T(1,128)S(1)} %broadcast_in_dim.15.gate_ref), custom_call_target="tpu_custom_call" | custom-call | tf_op jit(solution)/shard_map/combine/pallas_call | solution.py:263
  (5 shorter events, 0.0 us)
Async XLA Ops:
  0.0 7.8 %collective-permute-start = (bf16[128,1024]{1,0:T(8,128)(2,1)}, bf16[128,1024]{1,0:T(8,128)(2,1)S(1)}, u32[]{:S(2)}, u32[]{:S(2)}) collective-permute-start(bf16[128,1024]{1,0:T(8,128)(2,1)} %param.9), channel_id=1, source_target_pairs={{0,64},{16,80},{32,96},{48,112},{64,0},{80,16},{96,32},{112,48},{1... | collective-permute-start | bytes 786440 | tf_op jit(solution)/shard_map/ppermute | solution.py:23
  2.0 1.5 %copy-start = (bf16[1,1024,960]{1,2,0:T(8,128)(2,1)S(1)}, bf16[1,1024,960]{1,2,0:T(8,128)(2,1)}, u32[]{:S(2)}) copy-start(bf16[1,1024,960]{1,2,0:T(8,128)(2,1)} %param.11) | copy-start | bytes 5898244
  6.2 3.2 %copy-start.7 = (bf16[128,1024]{1,0:T(8,128)(2,1)S(1)}, bf16[128,1024]{1,0:T(8,128)(2,1)}, u32[]{:S(2)}) copy-start(bf16[128,1024]{1,0:T(8,128)(2,1)} %param.9) | copy-start | bytes 786436
  7.8 24.8 %collective-permute-start.5 = (f16[4,128,1024]{2,1,0:T(8,128)(2,1)}, f16[4,128,1024]{2,1,0:T(8,128)(2,1)S(1)}, u32[]{:S(2)}, u32[]{:S(2)}) collective-permute-start(f16[4,128,1024]{2,1,0:T(8,128)(2,1)} %multiply_convert_fusion), channel_id=1, source_target_pairs={{0,64},{16,80},{32,96},{48,112},{64,0},{80,16},{96,32},{112,48},{1... | collective-permute-start | bytes 3145736 | tf_op jit(solution)/shard_map/ppermute | solution.py:23
  9.5 12.9 %collective-permute-start.2 = (bf16[2,128,1024]{2,1,0:T(8,128)(2,1)S(1)}, bf16[2,128,1024]{2,1,0:T(8,128)(2,1)S(1)}, u32[]{:S(2)}, u32[]{:S(2)}) collective-permute-start(bf16[2,128,1024]{2,1,0:T(8,128)(2,1)S(1)} %pad_maximum_fusion.refs_0_), channel_id=1, source_target_pairs={{0,48},{16,0},{32,16},{48,32},{64,112},{80,64},{96,80},{112,96},{1... | collective-permute-start | bytes 1572872 | tf_op jit(solution)/shard_map/ppermute | solution.py:23
  12.3 12.5 %collective-permute-start.1 = (bf16[2,128,1024]{2,1,0:T(8,128)(2,1)S(1)}, bf16[2,128,1024]{2,1,0:T(8,128)(2,1)S(1)}, u32[]{:S(2)}, u32[]{:S(2)}) collective-permute-start(bf16[2,128,1024]{2,1,0:T(8,128)(2,1)S(1)} %pad_maximum_fusion.refs_0_), channel_id=1, source_target_pairs={{0,16},{16,32},{32,48},{48,0},{64,80},{80,96},{96,112},{112,64},{1... | collective-permute-start | bytes 1572872 | tf_op jit(solution)/shard_map/ppermute | solution.py:23
  15.3 13.2 %copy-start.8 = (s32[16,2]{0,1:T(2,128)S(1)}, s32[16,2]{0,1:T(2,128)}, u32[]{:S(2)}) copy-start(s32[16,2]{0,1:T(2,128)} %param.16) | copy-start | bytes 388
  25.6 7.0 %collective-permute-start.3 = (bf16[1,128,1024]{2,1,0:T(8,128)(2,1)}, bf16[1,128,1024]{2,1,0:T(8,128)(2,1)S(1)}, u32[]{:S(2)}, u32[]{:S(2)}) collective-permute-start(bf16[1,128,1024]{2,1,0:T(8,128)(2,1)} %slice.54), channel_id=1, source_target_pairs={{0,16},{16,32},{32,48},{48,0},{64,80},{80,96},{96,112},{112,64},{1... | collective-permute-start | bytes 786440 | tf_op jit(solution)/shard_map/ppermute | solution.py:23
  25.6 7.1 %collective-permute-start.4 = (bf16[1,128,1024]{2,1,0:T(8,128)(2,1)S(1)}, bf16[1,128,1024]{2,1,0:T(8,128)(2,1)S(1)}, u32[]{:S(2)}, u32[]{:S(2)}) collective-permute-start(bf16[1,128,1024]{2,1,0:T(8,128)(2,1)S(1)} %slice.55), channel_id=1, source_target_pairs={{0,48},{16,0},{32,16},{48,32},{64,112},{80,64},{96,80},{112,96},{1... | collective-permute-start | bytes 786440 | tf_op jit(solution)/shard_map/ppermute | solution.py:23
  28.2 29.0 %collective-permute-start.9 = (bf16[4,128,1024]{2,1,0:T(8,128)(2,1)}, bf16[4,128,1024]{2,1,0:T(8,128)(2,1)}, u32[]{:S(2)}, u32[]{:S(2)}) collective-permute-start(bf16[4,128,1024]{2,1,0:T(8,128)(2,1)} %get-tuple-element.32), channel_id=1, source_target_pairs={{0,64},{16,80},{32,96},{48,112},{64,0},{80,16},{96,32},{112,48},{1... | collective-permute-start | bytes 3145736 | tf_op jit(solution)/shard_map/ppermute | solution.py:23
  28.6 4.0 %copy-start.1 = (s32[16]{0:T(128)S(1)}, s32[16]{0:T(128)}, u32[]{:S(2)}) copy-start(s32[16]{0:T(128)} %slots_ref.3) | copy-start | bytes 196
  28.6 4.1 %copy-start.2 = (f32[128]{0:T(128)S(1)}, f32[128]{0:T(128)}, u32[]{:S(2)}) copy-start(f32[128]{0:T(128)} %param.13) | copy-start | bytes 1540
  32.6 4.9 %copy-start.5 = (f16[4,128,1024]{2,1,0:T(8,128)(2,1)}, f16[4,128,1024]{2,1,0:T(8,128)(2,1)S(1)}, u32[]{:S(2)}) copy-start(f16[4,128,1024]{2,1,0:T(8,128)(2,1)S(1)} %collective-permute-done.5) | copy-start | bytes 3145732
  32.6 4.9 %copy-start.3 = (f32[4,128,1024]{2,1,0:T(8,128)S(1)}, f32[4,128,1024]{2,1,0:T(8,128)}, u32[]{:S(2)}) copy-start(f32[4,128,1024]{2,1,0:T(8,128)} %get-tuple-element.29) | copy-start | bytes 6291460
  37.5 18.2 %copy-start.4 = (f32[4,128,1024]{2,1,0:T(8,128)S(1)}, f32[4,128,1024]{2,1,0:T(8,128)}, u32[]{:S(2)}) copy-start(f32[4,128,1024]{2,1,0:T(8,128)} %get-tuple-element.29) | copy-start | bytes 6291460
  38.6 17.1 %collective-permute-start.6 = (f16[128,1024]{1,0:T(8,128)(2,1)}, f16[128,1024]{1,0:T(8,128)(2,1)S(1)}, u32[]{:S(2)}, u32[]{:S(2)}) collective-permute-start(f16[128,1024]{1,0:T(8,128)(2,1)} %get-tuple-element.36), channel_id=1, source_target_pairs={{0,16},{16,32},{32,48},{48,0},{64,80},{80,96},{96,112},{112,64},{1... | collective-permute-start | bytes 786440 | tf_op jit(solution)/shard_map/ppermute | solution.py:23
  38.9 16.9 %collective-permute-start.8 = (f16[128,1024]{1,0:T(8,128)(2,1)}, f16[128,1024]{1,0:T(8,128)(2,1)}, u32[]{:S(2)}, u32[]{:S(2)}) collective-permute-start(f16[128,1024]{1,0:T(8,128)(2,1)} %get-tuple-element.37), channel_id=1, source_target_pairs={{0,32},{16,48},{32,0},{48,16},{64,96},{80,112},{96,64},{112,80},{1... | collective-permute-start | bytes 786440 | tf_op jit(solution)/shard_map/ppermute | solution.py:23
  41.5 14.2 %collective-permute-start.7 = (f16[128,1024]{1,0:T(8,128)(2,1)}, f16[128,1024]{1,0:T(8,128)(2,1)}, u32[]{:S(2)}, u32[]{:S(2)}) collective-permute-start(f16[128,1024]{1,0:T(8,128)(2,1)} %get-tuple-element.38), channel_id=1, source_target_pairs={{0,48},{16,0},{32,16},{48,32},{64,112},{80,64},{96,80},{112,96},{1... | collective-permute-start | bytes 786440 | tf_op jit(solution)/shard_map/ppermute | solution.py:23
  42.5 32.3 %all-to-all-start = ((bf16[16,32,1024]{2,1,0:T(8,128)(2,1)}), bf16[16,32,1024]{2,1,0:T(8,128)(2,1)S(1)}, u32[]{:S(2)}, u32[]{:S(2)}) async-start(bf16[16,32,1024]{2,1,0:T(8,128)(2,1)} %bitcast.7), calls=%async_computation | async-start | bytes 2097152 | tf_op jit(solution)/shard_map/all_to_all | solution.py:322
  55.7 6.3 %copy-start.9 = (f32[128]{0:T(128)S(1)}, f32[128]{0:T(128)}, u32[]{:S(2)}) copy-start(f32[128]{0:T(128)} %param.14) | copy-start | bytes 1540
  55.7 3.3 %copy-start.6 = (f16[128,1024]{1,0:T(8,128)(2,1)}, f16[128,1024]{1,0:T(8,128)(2,1)S(1)}, u32[]{:S(2)}) copy-start(f16[128,1024]{1,0:T(8,128)(2,1)S(1)} %collective-permute-done.6) | copy-start | bytes 786436
  59.1 14.1 %collective-permute-start.10 = (bf16[128,1024]{1,0:T(8,128)(2,1)S(1)}, bf16[128,1024]{1,0:T(8,128)(2,1)S(1)}, u32[]{:S(2)}, u32[]{:S(2)}) collective-permute-start(bf16[128,1024]{1,0:T(8,128)(2,1)S(1)} %get-tuple-element.33), channel_id=1, source_target_pairs={{0,16},{16,32},{32,48},{48,0},{64,80},{80,96},{96,112},{112,64},{1... | collective-permute-start | bytes 786440 | tf_op jit(solution)/shard_map/ppermute | solution.py:23
  59.5 13.7 %collective-permute-start.12 = (bf16[128,1024]{1,0:T(8,128)(2,1)S(1)}, bf16[128,1024]{1,0:T(8,128)(2,1)S(1)}, u32[]{:S(2)}, u32[]{:S(2)}) collective-permute-start(bf16[128,1024]{1,0:T(8,128)(2,1)S(1)} %get-tuple-element.34), channel_id=1, source_target_pairs={{0,32},{16,48},{32,0},{48,16},{64,96},{80,112},{96,64},{112,80},{1... | collective-permute-start | bytes 786440 | tf_op jit(solution)/shard_map/ppermute | solution.py:23
  60.1 13.5 %collective-permute-start.11 = (bf16[128,1024]{1,0:T(8,128)(2,1)S(1)}, bf16[128,1024]{1,0:T(8,128)(2,1)S(1)}, u32[]{:S(2)}, u32[]{:S(2)}) collective-permute-start(bf16[128,1024]{1,0:T(8,128)(2,1)S(1)} %get-tuple-element.35), channel_id=1, source_target_pairs={{0,48},{16,0},{32,16},{48,32},{64,112},{80,64},{96,80},{112,96},{1... | collective-permute-start | bytes 786440 | tf_op jit(solution)/shard_map/ppermute | solution.py:23
  80.6 27.3 %all-to-all-start.1 = ((bf16[16,32,1152]{2,1,0:T(8,128)(2,1)}), bf16[16,32,1152]{2,1,0:T(8,128)(2,1)S(1)}, u32[]{:S(2)}, u32[]{:S(2)}) async-start(bf16[16,32,1152]{2,1,0:T(8,128)(2,1)} %bitcast.17), calls=%async_computation.1 | async-start | bytes 2359296 | tf_op jit(solution)/shard_map/all_to_all | solution.py:343

commit v4 on v3

--- a/solution.py
+++ b/solution.py
@@ -289,10 +289,9 @@
 
     beside = permute(text_rows, 1, 0)
 
-    vision = features[0].T
+    vision = pltpu.with_memory_space_constraint(features[0].T, pltpu.HBM)
     (key_away,) = project(mine, kv_weight, vision, width, [(1, 0, jnp.float32)])
     key_away = (key_away * KEY_SCALE).astype(jnp.float16)
-    key_away, beside = lax.optimization_barrier((key_away, beside))
     key_away = permute(key_away, 1, 0)
 
     both_texts = jnp.stack([text_rows, beside])
@@ -309,7 +308,7 @@
         [(1, 1, jnp.bfloat16), (0, 0, jnp.float32), (0, 1, jnp.float32)],
         pltpu.HBM,
     )
-    before, behind, value_away = lax.optimization_barrier((before, behind, value_away))
+    before, value_away = lax.optimization_barrier((before, value_away))
     around = [permute(before[:1], 0, 1), permute(behind[1:], 0, RING - 1)]
     value_away = permute(value_away, 1, 0)
     places = [(0, -1), (1, -1), (0, 1), (1, 1)]

time: 110 us -> 107 us (0.973)
  waiting for transfers between devices: 30.8 us -> 27.1 us
  local copies, waits for them, and re-layouts: 2.41 us -> 0.87 us
  starting transfers between devices: 38.1 us -> 39.6 us
  Pallas kernels: 29 us -> 30.2 us
    ppermute x13, waiting for transfers between devices: 12.8 us -> 7.72 us  [permute(): return lax.ppermute(values, 'feat', pairs)]
    all_to_all x1, starting transfers between devices: 8.62 us -> 10.8 us  [per_device(): lax.all_to_all(back.reshape(images, CAP * words, columns + width), 'dp',...]
    unnamed x21 -> x19, local copies, waits for them, and re-layouts: 1.67 us -> 0.12 us
    all_to_all x1, starting transfers between devices: 13.2 us -> 11.7 us  [per_device(): lax.all_to_all(sent.reshape(images, CAP * words, columns), 'dp', 0, 0, ti...]
    all_to_all x1, waiting for transfers between devices: 0.01 us -> 1.43 us  [per_device(): lax.all_to_all(sent.reshape(images, CAP * words, columns), 'dp', 0, 0, ti...]
    pallas_call x2, Pallas kernels: 9.7 us -> 10.8 us  [project(): pl.pallas_call(functools.partial(project_kernel, outs=len(outs)), grid_sp...]
  transfers between devices with their start and end apart: 15 -> 15, of which waited for: 5 -> 7; matrix products, arithmetic and copies ran while one was open for 8% -> 9% of each run, Pallas kernels for 20% -> 21%
where the time goes in v4:
time: 107 us
  starting transfers between devices  39.6 us (37%)
  Pallas kernels  30.2 us (28%)
  waiting for transfers between devices  27.1 us (25%)
  other arithmetic  8.39 us (8%)
    all_to_all x1, waiting for transfers between devices, per_device(): lax.all_to_all(back.reshape(images, CAP * words, columns + width), 'dp',...  18 us
    ppermute x13, starting transfers between devices, permute(): return lax.ppermute(values, 'feat', pairs)  17.1 us
    all_to_all x1, starting transfers between devices, per_device(): lax.all_to_all(sent.reshape(images, CAP * words, columns), 'dp', 0, 0, ti...  11.7 us
    pallas_call x2, Pallas kernels, project(): pl.pallas_call(functools.partial(project_kernel, outs=len(outs)), grid_sp...  10.8 us
    all_to_all x1, starting transfers between devices, per_device(): lax.all_to_all(back.reshape(images, CAP * words, columns + width), 'dp',...  10.8 us
    ppermute x13, waiting for transfers between devices, permute(): return lax.ppermute(values, 'feat', pairs)  7.72 us
    pallas_call x2, Pallas kernels, query_step(): pl.pallas_call(functools.partial(query_step_kernel, places=places, first=...  6.96 us
    pallas_call x1, Pallas kernels, attend(): pl.pallas_call(attend_kernel, in_specs=[vmem] * 3, out_specs=vmem, out_sh...  5.71 us
  transfers between devices with their start and end apart: 15, of which 7 were waited for; matrix products, arithmetic and copies ran while one was open for 9% of the time, Pallas kernels for 21%

profile of v4, /device:TPU:1, one launch (start us, length us, event | category | flops | bytes accessed | tf_op | source)
XLA Modules:
  0.0 107.0 jit_solution(11542664837409731769)
XLA Ops:
  0.0 2.0 %collective-permute-start = (bf16[128,1024]{1,0:T(8,128)(2,1)}, bf16[128,1024]{1,0:T(8,128)(2,1)S(1)}, u32[]{:S(2)}, u32[]{:S(2)}) collective-permute-start(bf16[128,1024]{1,0:T(8,128)(2,1)} %param.9), channel_id=1, source_target_pairs={{0,64},{16,80},{32,96},{48,112},{64,0},{80,16},{96,32},{112,48},{1... | collective-permute-start | bytes 786440 | tf_op jit(solution)/shard_map/ppermute | solution.py:23
  2.0 3.3 %project.3 = f32[4,128,1024]{2,1,0:T(8,128)S(1)} custom-call(s32[1]{0:T(128)} %bitcast.mine._, bf16[960,2048]{1,0:T(8,128)(2,1)} %refs_3_.3, bf16[960,2048]{1,0:T(8,128)(2,1)} %refs_3_.3, bf16[960,2048]{1,0:T(8,128)(2,1)} %refs_3_.3, bf16[960,2048]{1,0:T(8,128)(2,1)} %refs_3_.3, bf16[960,1024]{1,0:T(8,128)(2,1)} %bitcast.46), custom_call_target="tpu_custom_call" | custom-call | tf_op jit(solution)/shard_map/project/pallas_call | solution.py:48
  5.4 0.0 copy-start.6
  5.4 1.3 %multiply_convert_fusion = f16[4,128,1024]{2,1,0:T(8,128)(2,1)} fusion(f32[4,128,1024]{2,1,0:T(8,128)S(1)} %project.3), kind=kLoop, calls=%fused_computation | loop fusion | flops 1048576 | bytes 3145728 | tf_op jit(solution)/shard_map/convert_element_type | solution.py:294
  6.6 0.0 collective-permute-start.5
  6.6 1.1 %collective-permute-done = bf16[128,1024]{1,0:T(8,128)(2,1)S(1)} collective-permute-done((bf16[128,1024]{1,0:T(8,128)(2,1)}, bf16[128,1024]{1,0:T(8,128)(2,1)S(1)}, u32[]{:S(2)}, u32[]{:S(2)}) %collective-permute-start) | collective-permute-done | bytes 262176 | tf_op jit(solution)/shard_map/ppermute | solution.py:23
  7.8 0.0 copy-done.6
  7.8 0.1 pad_maximum_fusion.refs_0_
  7.8 1.8 %collective-permute-start.1 = (bf16[2,128,1024]{2,1,0:T(8,128)(2,1)S(1)}, bf16[2,128,1024]{2,1,0:T(8,128)(2,1)S(1)}, u32[]{:S(2)}, u32[]{:S(2)}) collective-permute-start(bf16[2,128,1024]{2,1,0:T(8,128)(2,1)S(1)} %pad_maximum_fusion.refs_0_), channel_id=1, source_target_pairs={{0,16},{16,32},{32,48},{48,0},{64,80},{80,96},{96,112},{112,64},{1... | collective-permute-start | bytes 1572872 | tf_op jit(solution)/shard_map/ppermute | solution.py:23
  9.6 1.5 %collective-permute-start.3 = (bf16[2,128,1024]{2,1,0:T(8,128)(2,1)S(1)}, bf16[2,128,1024]{2,1,0:T(8,128)(2,1)S(1)}, u32[]{:S(2)}, u32[]{:S(2)}) collective-permute-start(bf16[2,128,1024]{2,1,0:T(8,128)(2,1)S(1)} %pad_maximum_fusion.refs_0_), channel_id=1, source_target_pairs={{0,48},{16,0},{32,16},{48,32},{64,112},{80,64},{96,80},{112,96},{1... | collective-permute-start | bytes 1572872 | tf_op jit(solution)/shard_map/ppermute | solution.py:23
  11.2 3.0 %query_step.2.refs_3_ = f32[128,1024]{1,0:T(8,128)S(1)} custom-call(s32[1]{0:T(128)} %bitcast.mine._, bf16[2,128,1024]{2,1,0:T(8,128)(2,1)S(1)} %pad_maximum_fusion.refs_0_, bf16[8192,1024]{1,0:T(8,128)(2,1)} %refs_2_.7), custom_call_target="tpu_custom_call" | custom-call | tf_op jit(solution)/shard_map/query_step/pallas_call | solution.py:107
  14.1 0.0 copy-start.7
  14.1 7.5 %project.2 = (bf16[4,128,1024]{2,1,0:T(8,128)(2,1)}, f32[4,128,1024]{2,1,0:T(8,128)}, f32[4,128,1024]{2,1,0:T(8,128)}) custom-call(s32[1]{0:T(128)} %bitcast.mine._, bf16[960,2048]{1,0:T(8,128)(2,1)} %refs_3_.3, bf16[960,2048]{1,0:T(8,128)(2,1)} %refs_3_.3, bf16[960,2048]{1,0:T(8,128)(2,1)} %refs_3_.3, bf16[960,2048]{1,0:T(8,128)(2,1)} %refs_3_.3, ...), custom_call_target="tpu_custom_call" | custom-call | tf_op jit(solution)/shard_map/project/pallas_call | solution.py:48
  21.6 0.0 collective-permute-done.1.refs_0_
  21.7 0.1 collective-permute-start.2
  21.8 0.0 collective-permute-done.3.refs_1_
  21.8 0.7 slice.72
  22.5 2.7 %collective-permute-start.4 = (bf16[1,128,1024]{2,1,0:T(8,128)(2,1)}, bf16[1,128,1024]{2,1,0:T(8,128)(2,1)S(1)}, u32[]{:S(2)}, u32[]{:S(2)}) collective-permute-start(bf16[1,128,1024]{2,1,0:T(8,128)(2,1)} %slice.72), channel_id=1, source_target_pairs={{0,48},{16,0},{32,16},{48,32},{64,112},{80,64},{96,80},{112,96},{1... | collective-permute-start | bytes 786440 | tf_op jit(solution)/shard_map/ppermute | solution.py:23
  25.1 1.2 %collective-permute-start.9 = (bf16[4,128,1024]{2,1,0:T(8,128)(2,1)}, bf16[4,128,1024]{2,1,0:T(8,128)(2,1)}, u32[]{:S(2)}, u32[]{:S(2)}) collective-permute-start(bf16[4,128,1024]{2,1,0:T(8,128)(2,1)} %get-tuple-element.26), channel_id=1, source_target_pairs={{0,64},{16,80},{32,96},{48,112},{64,0},{80,16},{96,32},{112,48},{1... | collective-permute-start | bytes 3145736 | tf_op jit(solution)/shard_map/ppermute | solution.py:23
  26.4 0.0 copy-done.7
  26.4 0.1 copy.11.ids_ref
  26.4 0.0 copy-start
  26.4 0.0 copy-start.1
  26.4 4.0 %query_step.3.refs_3_ = f32[128,1024]{1,0:T(8,128)S(1)} custom-call(s32[1]{0:T(128)} %bitcast.mine._, bf16[2,128,1024]{2,1,0:T(8,128)(2,1)S(1)} %collective-permute-done.1.refs_0_, bf16[2,128,1024]{2,1,0:T(8,128)(2,1)S(1)} %collective-permute-done.3.refs_1_, bf16[8192,1024]{1,0:T(8,128)(2,1)} %refs_2_.7, f32[128,1024]{1,0:T(8,128)S(1)} %query_step.2.refs_3_), custom_call_target="tpu_custom_call" | custom-call | tf_op jit(solution)/shard_map/query_step/pallas_call | solution.py:107
  30.4 0.1 collective-permute-done.5
  30.5 0.0 copy-start.4
  30.5 0.0 collective-permute-done.2.refs_0_
  30.5 0.0 collective-permute-done.4.refs_1_
  30.6 0.0 copy-done
  30.6 0.0 copy-done.1
  30.6 0.0 copy-start.2
  30.6 4.9 %query_last.1 = bf16[512,1024]{1,0:T(8,128)(2,1)} custom-call(s32[1]{0:T(128)} %bitcast.mine._, s32[16,2]{1,0:T(8,128)S(1)} %copy.11.ids_ref, s32[16]{0:T(128)S(1)} %copy-done, bf16[1,128,1024]{2,1,0:T(8,128)(2,1)S(1)} %collective-permute-done.2.refs_0_, bf16[1,128,1024]{2,1,0:T(8,128)(2,1)S(1)} %collective-permute-done.4.refs_1_, ...), custom_call_target="tpu_custom_call" | custom-call | tf_op jit(solution)/shard_map/query_last/pallas_call | solution.py:173
  35.5 0.0 copy-done.4
  35.5 0.0 copy-done.2
  35.5 0.0 copy-start.3
  35.5 1.0 fusion.5
  36.6 1.3 %collective-permute-start.6 = (f16[128,1024]{1,0:T(8,128)(2,1)}, f16[128,1024]{1,0:T(8,128)(2,1)S(1)}, u32[]{:S(2)}, u32[]{:S(2)}) collective-permute-start(f16[128,1024]{1,0:T(8,128)(2,1)} %get-tuple-element.30), channel_id=1, source_target_pairs={{0,16},{16,32},{32,48},{48,0},{64,80},{80,96},{96,112},{112,64},{1... | collective-permute-start | bytes 786440 | tf_op jit(solution)/shard_map/ppermute | solution.py:23
  37.9 1.4 %collective-permute-start.7 = (f16[128,1024]{1,0:T(8,128)(2,1)}, f16[128,1024]{1,0:T(8,128)(2,1)}, u32[]{:S(2)}, u32[]{:S(2)}) collective-permute-start(f16[128,1024]{1,0:T(8,128)(2,1)} %get-tuple-element.32), channel_id=1, source_target_pairs={{0,48},{16,0},{32,16},{48,32},{64,112},{80,64},{96,80},{112,96},{1... | collective-permute-start | bytes 786440 | tf_op jit(solution)/shard_map/ppermute | solution.py:23
  39.3 1.6 %collective-permute-start.8 = (f16[128,1024]{1,0:T(8,128)(2,1)}, f16[128,1024]{1,0:T(8,128)(2,1)}, u32[]{:S(2)}, u32[]{:S(2)}) collective-permute-start(f16[128,1024]{1,0:T(8,128)(2,1)} %get-tuple-element.31), channel_id=1, source_target_pairs={{0,32},{16,48},{32,0},{48,16},{64,96},{80,112},{96,64},{112,80},{1... | collective-permute-start | bytes 786440 | tf_op jit(solution)/shard_map/ppermute | solution.py:23
  41.0 11.7 %all-to-all-start = ((bf16[16,32,1024]{2,1,0:T(8,128)(2,1)}), bf16[16,32,1024]{2,1,0:T(8,128)(2,1)S(1)}, u32[]{:S(2)}, u32[]{:S(2)}) async-start(bf16[16,32,1024]{2,1,0:T(8,128)(2,1)} %bitcast.7), calls=%async_computation | async-start | bytes 2097152 | tf_op jit(solution)/shard_map/all_to_all | solution.py:321
  52.6 0.0 copy-start.8
  52.6 0.0 collective-permute-done.6
  52.6 0.0 copy-start.5
  52.6 0.0 collective-permute-done.7
  52.7 0.0 collective-permute-done.8
  52.7 0.0 copy-done.3
  52.7 1.4 %multiply_reduce_fusion = f32[1024]{0:T(1024)S(1)} fusion(f16[128,1024]{1,0:T(8,128)(2,1)} %collective-permute-done.8, f16[128,1024]{1,0:T(8,128)(2,1)} %collective-permute-done.7, f16[128,1024]{1,0:T(8,128)(2,1)S(1)} %collective-permute-done.6, f16[4,128,1024]{2,1,0:T(8,128)(2,1)} %copy-done.4, f32[4,128,1024]{2,1,0:T(8,128)S(1)} %copy-done.3), kind=kLoop, calls=%fused_computation.13 | loop fusion | flops 1440768 | bytes 1576960 | tf_op jit(solution)/shard_map/reduce_sum | solution.py:335
  54.1 0.0 collective-permute-done.9
  54.1 1.8 %fusion.8 = (bf16[128,1024]{1,0:T(8,128)(2,1)S(1)}, bf16[128,1024]{1,0:T(8,128)(2,1)S(1)}, bf16[128,1024]{1,0:T(8,128)(2,1)S(1)}) fusion(f32[4,128,1024]{2,1,0:T(8,128)} %get-tuple-element.25, bf16[4,128,1024]{2,1,0:T(8,128)(2,1)} %collective-permute-done.9), kind=kLoop, calls=%fused_computation.20 | loop fusion | flops 1179648 | bytes 3145728 | tf_op jit(solution)/shard_map/convert_element_type | solution.py:329
  56.0 0.0 copy-done.5
  56.0 0.5 collective-permute-start.10
  56.5 2.3 %collective-permute-start.11 = (bf16[128,1024]{1,0:T(8,128)(2,1)S(1)}, bf16[128,1024]{1,0:T(8,128)(2,1)S(1)}, u32[]{:S(2)}, u32[]{:S(2)}) collective-permute-start(bf16[128,1024]{1,0:T(8,128)(2,1)S(1)} %get-tuple-element.29), channel_id=1, source_target_pairs={{0,48},{16,0},{32,16},{48,32},{64,112},{80,64},{96,80},{112,96},{1... | collective-permute-start | bytes 786440 | tf_op jit(solution)/shard_map/ppermute | solution.py:23
  58.7 0.7 collective-permute-start.12
  59.4 0.0 copy-done.8
  59.4 1.5 %multiply_convert_fusion.1.key_ref = bf16[128,1024]{1,0:T(8,128)(2,1)S(1)} fusion(f32[128]{0:T(128)S(1)} %copy-done.8, f32[1024]{0:T(1024)S(1)} %add_rsqrt_fusion, f16[128,1024]{1,0:T(8,128)(2,1)} %collective-permute-done.8, f16[128,1024]{1,0:T(8,128)(2,1)} %collective-permute-done.7, f16[128,1024]{1,0:T(8,128)(2,1)} %copy-done.5, ...), kind=kLoop, calls=%fused_computation.12 | loop fusion | flops 1572864 | bytes 1839616 | tf_op jit(solution)/shard_map/convert_element_type | solution.py:338
  60.9 2.1 %collective-permute-done.10 = bf16[128,1024]{1,0:T(8,128)(2,1)S(1)} collective-permute-done((bf16[128,1024]{1,0:T(8,128)(2,1)S(1)}, bf16[128,1024]{1,0:T(8,128)(2,1)S(1)}, u32[]{:S(2)}, u32[]{:S(2)}) %collective-permute-start.10) | collective-permute-done | bytes 262176 | tf_op jit(solution)/shard_map/ppermute | solution.py:23
  63.0 2.5 %collective-permute-done.11 = bf16[128,1024]{1,0:T(8,128)(2,1)S(1)} collective-permute-done((bf16[128,1024]{1,0:T(8,128)(2,1)S(1)}, bf16[128,1024]{1,0:T(8,128)(2,1)S(1)}, u32[]{:S(2)}, u32[]{:S(2)}) %collective-permute-start.11) | collective-permute-done | bytes 262176 | tf_op jit(solution)/shard_map/ppermute | solution.py:23
  65.5 1.9 %collective-permute-done.12 = bf16[128,1024]{1,0:T(8,128)(2,1)S(1)} collective-permute-done((bf16[128,1024]{1,0:T(8,128)(2,1)S(1)}, bf16[128,1024]{1,0:T(8,128)(2,1)S(1)}, u32[]{:S(2)}, u32[]{:S(2)}) %collective-permute-start.12) | collective-permute-done | bytes 262176 | tf_op jit(solution)/shard_map/ppermute | solution.py:23
  67.3 1.3 %fusion.2.value_ref = bf16[128,1024]{1,0:T(8,128)(2,1)S(1)} fusion(bf16[128,1024]{1,0:T(8,128)(2,1)S(1)} %collective-permute-done.12, bf16[128,1024]{1,0:T(8,128)(2,1)S(1)} %collective-permute-done.11, bf16[128,1024]{1,0:T(8,128)(2,1)S(1)} %collective-permute-done.10, f32[4,128,1024]{2,1,0:T(8,128)} %get-tuple-element.25, ...), kind=kLoop, calls=%fused_computation.5 | loop fusion | flops 1179648 | bytes 1835008 | tf_op jit(solution)/shard_map/convert_element_type | solution.py:339
  68.6 1.4 %all-to-all-done = bf16[16,32,1024]{2,1,0:T(8,128)(2,1)S(1)} async-done(((bf16[16,32,1024]{2,1,0:T(8,128)(2,1)}), bf16[16,32,1024]{2,1,0:T(8,128)(2,1)S(1)}, u32[]{:S(2)}, u32[]{:S(2)}) %all-to-all-start) | async-done | bytes 1048608 | tf_op jit(solution)/shard_map/all_to_all | solution.py:321
  70.1 5.7 %attend.1 = bf16[512,1152]{1,0:T(8,128)(2,1)} custom-call(bf16[512,1024]{1,0:T(8,128)(2,1)S(1)} %bitcast.44, bf16[128,1024]{1,0:T(8,128)(2,1)S(1)} %multiply_convert_fusion.1.key_ref, bf16[128,1024]{1,0:T(8,128)(2,1)S(1)} %fusion.2.value_ref), custom_call_target="tpu_custom_call" | custom-call | tf_op jit(solution)/shard_map/attend/pallas_call | solution.py:218
  75.8 10.8 %all-to-all-start.1 = ((bf16[16,32,1152]{2,1,0:T(8,128)(2,1)}), bf16[16,32,1152]{2,1,0:T(8,128)(2,1)S(1)}, u32[]{:S(2)}, u32[]{:S(2)}) async-start(bf16[16,32,1152]{2,1,0:T(8,128)(2,1)} %bitcast.17), calls=%async_computation.1 | async-start | bytes 2359296 | tf_op jit(solution)/shard_map/all_to_all | solution.py:342
  87.2 18.0 %all-to-all-done.1 = bf16[16,32,1152]{2,1,0:T(8,128)(2,1)S(1)} async-done(((bf16[16,32,1152]{2,1,0:T(8,128)(2,1)}), bf16[16,32,1152]{2,1,0:T(8,128)(2,1)S(1)}, u32[]{:S(2)}, u32[]{:S(2)}) %all-to-all-start.1) | async-done | bytes 1179680 | tf_op jit(solution)/shard_map/all_to_all | solution.py:342
  105.2 1.8 %combine.1 = bf16[128,1024]{1,0:T(8,128)(2,1)} custom-call(s32[16,2]{1,0:T(8,128)S(1)} %copy.11.ids_ref, s32[16]{0:T(128)S(1)} %copy-done, bf16[512,1152]{1,0:T(8,128)(2,1)S(1)} %bitcast.43, f32[1,128]{1,0:T(1,128)S(1)} %broadcast_in_dim.15.gate_ref), custom_call_target="tpu_custom_call" | custom-call | tf_op jit(solution)/shard_map/combine/pallas_call | solution.py:263
  (3 shorter events, 0.0 us)
Async XLA Ops:
  0.0 7.8 %collective-permute-start = (bf16[128,1024]{1,0:T(8,128)(2,1)}, bf16[128,1024]{1,0:T(8,128)(2,1)S(1)}, u32[]{:S(2)}, u32[]{:S(2)}) collective-permute-start(bf16[128,1024]{1,0:T(8,128)(2,1)} %param.9), channel_id=1, source_target_pairs={{0,64},{16,80},{32,96},{48,112},{64,0},{80,16},{96,32},{112,48},{1... | collective-permute-start | bytes 786440 | tf_op jit(solution)/shard_map/ppermute | solution.py:23
  5.4 2.4 %copy-start.6 = (bf16[128,1024]{1,0:T(8,128)(2,1)S(1)}, bf16[128,1024]{1,0:T(8,128)(2,1)}, u32[]{:S(2)}) copy-start(bf16[128,1024]{1,0:T(8,128)(2,1)} %param.9) | copy-start | bytes 786436
  6.6 23.9 %collective-permute-start.5 = (f16[4,128,1024]{2,1,0:T(8,128)(2,1)}, f16[4,128,1024]{2,1,0:T(8,128)(2,1)S(1)}, u32[]{:S(2)}, u32[]{:S(2)}) collective-permute-start(f16[4,128,1024]{2,1,0:T(8,128)(2,1)} %multiply_convert_fusion), channel_id=1, source_target_pairs={{0,64},{16,80},{32,96},{48,112},{64,0},{80,16},{96,32},{112,48},{1... | collective-permute-start | bytes 3145736 | tf_op jit(solution)/shard_map/ppermute | solution.py:23
  7.8 13.8 %collective-permute-start.1 = (bf16[2,128,1024]{2,1,0:T(8,128)(2,1)S(1)}, bf16[2,128,1024]{2,1,0:T(8,128)(2,1)S(1)}, u32[]{:S(2)}, u32[]{:S(2)}) collective-permute-start(bf16[2,128,1024]{2,1,0:T(8,128)(2,1)S(1)} %pad_maximum_fusion.refs_0_), channel_id=1, source_target_pairs={{0,16},{16,32},{32,48},{48,0},{64,80},{80,96},{96,112},{112,64},{1... | collective-permute-start | bytes 1572872 | tf_op jit(solution)/shard_map/ppermute | solution.py:23
  9.6 12.1 %collective-permute-start.3 = (bf16[2,128,1024]{2,1,0:T(8,128)(2,1)S(1)}, bf16[2,128,1024]{2,1,0:T(8,128)(2,1)S(1)}, u32[]{:S(2)}, u32[]{:S(2)}) collective-permute-start(bf16[2,128,1024]{2,1,0:T(8,128)(2,1)S(1)} %pad_maximum_fusion.refs_0_), channel_id=1, source_target_pairs={{0,48},{16,0},{32,16},{48,32},{64,112},{80,64},{96,80},{112,96},{1... | collective-permute-start | bytes 1572872 | tf_op jit(solution)/shard_map/ppermute | solution.py:23
  14.1 12.2 %copy-start.7 = (s32[16,2]{0,1:T(2,128)S(1)}, s32[16,2]{0,1:T(2,128)}, u32[]{:S(2)}) copy-start(s32[16,2]{0,1:T(2,128)} %param.16) | copy-start | bytes 388
  21.7 8.9 %collective-permute-start.2 = (bf16[1,128,1024]{2,1,0:T(8,128)(2,1)S(1)}, bf16[1,128,1024]{2,1,0:T(8,128)(2,1)S(1)}, u32[]{:S(2)}, u32[]{:S(2)}) collective-permute-start(bf16[1,128,1024]{2,1,0:T(8,128)(2,1)S(1)} %slice.54), channel_id=1, source_target_pairs={{0,16},{16,32},{32,48},{48,0},{64,80},{80,96},{96,112},{112,64},{1... | collective-permute-start | bytes 786440 | tf_op jit(solution)/shard_map/ppermute | solution.py:23
  22.5 8.1 %collective-permute-start.4 = (bf16[1,128,1024]{2,1,0:T(8,128)(2,1)}, bf16[1,128,1024]{2,1,0:T(8,128)(2,1)S(1)}, u32[]{:S(2)}, u32[]{:S(2)}) collective-permute-start(bf16[1,128,1024]{2,1,0:T(8,128)(2,1)} %slice.72), channel_id=1, source_target_pairs={{0,48},{16,0},{32,16},{48,32},{64,112},{80,64},{96,80},{112,96},{1... | collective-permute-start | bytes 786440 | tf_op jit(solution)/shard_map/ppermute | solution.py:23
  25.1 29.0 %collective-permute-start.9 = (bf16[4,128,1024]{2,1,0:T(8,128)(2,1)}, bf16[4,128,1024]{2,1,0:T(8,128)(2,1)}, u32[]{:S(2)}, u32[]{:S(2)}) collective-permute-start(bf16[4,128,1024]{2,1,0:T(8,128)(2,1)} %get-tuple-element.26), channel_id=1, source_target_pairs={{0,64},{16,80},{32,96},{48,112},{64,0},{80,16},{96,32},{112,48},{1... | collective-permute-start | bytes 3145736 | tf_op jit(solution)/shard_map/ppermute | solution.py:23
  26.4 4.1 %copy-start = (s32[16]{0:T(128)S(1)}, s32[16]{0:T(128)}, u32[]{:S(2)}) copy-start(s32[16]{0:T(128)} %slots_ref.3) | copy-start | bytes 196
  26.4 4.1 %copy-start.1 = (f32[128]{0:T(128)S(1)}, f32[128]{0:T(128)}, u32[]{:S(2)}) copy-start(f32[128]{0:T(128)} %param.13) | copy-start | bytes 1540
  30.5 5.0 %copy-start.4 = (f16[4,128,1024]{2,1,0:T(8,128)(2,1)}, f16[4,128,1024]{2,1,0:T(8,128)(2,1)S(1)}, u32[]{:S(2)}) copy-start(f16[4,128,1024]{2,1,0:T(8,128)(2,1)S(1)} %collective-permute-done.5) | copy-start | bytes 3145732
  30.6 4.9 %copy-start.2 = (f32[4,128,1024]{2,1,0:T(8,128)S(1)}, f32[4,128,1024]{2,1,0:T(8,128)}, u32[]{:S(2)}) copy-start(f32[4,128,1024]{2,1,0:T(8,128)} %get-tuple-element.23) | copy-start | bytes 6291460
  35.5 17.2 %copy-start.3 = (f32[4,128,1024]{2,1,0:T(8,128)S(1)}, f32[4,128,1024]{2,1,0:T(8,128)}, u32[]{:S(2)}) copy-start(f32[4,128,1024]{2,1,0:T(8,128)} %get-tuple-element.23) | copy-start | bytes 6291460
  36.6 16.1 %collective-permute-start.6 = (f16[128,1024]{1,0:T(8,128)(2,1)}, f16[128,1024]{1,0:T(8,128)(2,1)S(1)}, u32[]{:S(2)}, u32[]{:S(2)}) collective-permute-start(f16[128,1024]{1,0:T(8,128)(2,1)} %get-tuple-element.30), channel_id=1, source_target_pairs={{0,16},{16,32},{32,48},{48,0},{64,80},{80,96},{96,112},{112,64},{1... | collective-permute-start | bytes 786440 | tf_op jit(solution)/shard_map/ppermute | solution.py:23
  37.9 14.8 %collective-permute-start.7 = (f16[128,1024]{1,0:T(8,128)(2,1)}, f16[128,1024]{1,0:T(8,128)(2,1)}, u32[]{:S(2)}, u32[]{:S(2)}) collective-permute-start(f16[128,1024]{1,0:T(8,128)(2,1)} %get-tuple-element.32), channel_id=1, source_target_pairs={{0,48},{16,0},{32,16},{48,32},{64,112},{80,64},{96,80},{112,96},{1... | collective-permute-start | bytes 786440 | tf_op jit(solution)/shard_map/ppermute | solution.py:23
  39.3 13.4 %collective-permute-start.8 = (f16[128,1024]{1,0:T(8,128)(2,1)}, f16[128,1024]{1,0:T(8,128)(2,1)}, u32[]{:S(2)}, u32[]{:S(2)}) collective-permute-start(f16[128,1024]{1,0:T(8,128)(2,1)} %get-tuple-element.31), channel_id=1, source_target_pairs={{0,32},{16,48},{32,0},{48,16},{64,96},{80,112},{96,64},{112,80},{1... | collective-permute-start | bytes 786440 | tf_op jit(solution)/shard_map/ppermute | solution.py:23
  41.0 29.1 %all-to-all-start = ((bf16[16,32,1024]{2,1,0:T(8,128)(2,1)}), bf16[16,32,1024]{2,1,0:T(8,128)(2,1)S(1)}, u32[]{:S(2)}, u32[]{:S(2)}) async-start(bf16[16,32,1024]{2,1,0:T(8,128)(2,1)} %bitcast.7), calls=%async_computation | async-start | bytes 2097152 | tf_op jit(solution)/shard_map/all_to_all | solution.py:321
  52.6 6.8 %copy-start.8 = (f32[128]{0:T(128)S(1)}, f32[128]{0:T(128)}, u32[]{:S(2)}) copy-start(f32[128]{0:T(128)} %param.14) | copy-start | bytes 1540
  52.6 3.3 %copy-start.5 = (f16[128,1024]{1,0:T(8,128)(2,1)}, f16[128,1024]{1,0:T(8,128)(2,1)S(1)}, u32[]{:S(2)}) copy-start(f16[128,1024]{1,0:T(8,128)(2,1)S(1)} %collective-permute-done.6) | copy-start | bytes 786436
  56.0 7.0 %collective-permute-start.10 = (bf16[128,1024]{1,0:T(8,128)(2,1)S(1)}, bf16[128,1024]{1,0:T(8,128)(2,1)S(1)}, u32[]{:S(2)}, u32[]{:S(2)}) collective-permute-start(bf16[128,1024]{1,0:T(8,128)(2,1)S(1)} %get-tuple-element.27), channel_id=1, source_target_pairs={{0,16},{16,32},{32,48},{48,0},{64,80},{80,96},{96,112},{112,64},{1... | collective-permute-start | bytes 786440 | tf_op jit(solution)/shard_map/ppermute | solution.py:23
  56.5 9.0 %collective-permute-start.11 = (bf16[128,1024]{1,0:T(8,128)(2,1)S(1)}, bf16[128,1024]{1,0:T(8,128)(2,1)S(1)}, u32[]{:S(2)}, u32[]{:S(2)}) collective-permute-start(bf16[128,1024]{1,0:T(8,128)(2,1)S(1)} %get-tuple-element.29), channel_id=1, source_target_pairs={{0,48},{16,0},{32,16},{48,32},{64,112},{80,64},{96,80},{112,96},{1... | collective-permute-start | bytes 786440 | tf_op jit(solution)/shard_map/ppermute | solution.py:23
  58.7 8.6 %collective-permute-start.12 = (bf16[128,1024]{1,0:T(8,128)(2,1)S(1)}, bf16[128,1024]{1,0:T(8,128)(2,1)S(1)}, u32[]{:S(2)}, u32[]{:S(2)}) collective-permute-start(bf16[128,1024]{1,0:T(8,128)(2,1)S(1)} %get-tuple-element.28), channel_id=1, source_target_pairs={{0,32},{16,48},{32,0},{48,16},{64,96},{80,112},{96,64},{112,80},{1... | collective-permute-start | bytes 786440 | tf_op jit(solution)/shard_map/ppermute | solution.py:23
  75.8 29.4 %all-to-all-start.1 = ((bf16[16,32,1152]{2,1,0:T(8,128)(2,1)}), bf16[16,32,1152]{2,1,0:T(8,128)(2,1)S(1)}, u32[]{:S(2)}, u32[]{:S(2)}) async-start(bf16[16,32,1152]{2,1,0:T(8,128)(2,1)} %bitcast.17), calls=%async_computation.1 | async-start | bytes 2359296 | tf_op jit(solution)/shard_map/all_to_all | solution.py:342

commit v5 on v4

--- a/solution.py
+++ b/solution.py
@@ -39,7 +39,7 @@
     return ((mine[0] // RING) ^ across) * RING + ((mine[0] + along) & (RING - 1))
 
 
-def project(mine, kv_weight, vision, width, outs, shape=jax.ShapeDtypeStruct):
+def project(mine, kv_weight, vision, width, outs, parts, shape=jax.ShapeDtypeStruct):
     depth, tokens = vision.shape
 
     def block(across, part, along, _, mine):
@@ -49,14 +49,14 @@
         functools.partial(project_kernel, outs=len(outs)),
         grid_spec=pltpu.PrefetchScalarGridSpec(
             num_scalar_prefetch=1,
-            grid=(1,),
+            grid=(parts,),
             in_specs=[
                 pl.BlockSpec((depth, width), functools.partial(block, across, part, along))
                 for across, part, _ in outs
                 for along in range(RING)
             ]
-            + [pl.BlockSpec((depth, tokens), lambda g, m: (0, 0))],
-            out_specs=[pl.BlockSpec((RING, width, tokens), lambda g, m: (0, 0, 0))] * len(outs),
+            + [pl.BlockSpec((depth, tokens // parts), lambda g, m: (0, g))],
+            out_specs=[pl.BlockSpec((RING, width, tokens // parts), lambda g, m: (0, 0, g))] * len(outs),
         ),
         out_shape=[shape((RING, width, tokens), kind) for _, _, kind in outs],
         compiler_params=pltpu.CompilerParams(vmem_limit_bytes=24 << 20),
@@ -290,7 +290,7 @@
     beside = permute(text_rows, 1, 0)
 
     vision = pltpu.with_memory_space_constraint(features[0].T, pltpu.HBM)
-    (key_away,) = project(mine, kv_weight, vision, width, [(1, 0, jnp.float32)])
+    (key_away,) = project(mine, kv_weight, vision, width, [(1, 0, jnp.float32)], 1)
     key_away = (key_away * KEY_SCALE).astype(jnp.float16)
     key_away = permute(key_away, 1, 0)
 
@@ -306,6 +306,7 @@
         vision,
         width,
         [(1, 1, jnp.bfloat16), (0, 0, jnp.float32), (0, 1, jnp.float32)],
+        2,
         pltpu.HBM,
     )
     before, value_away = lax.optimization_barrier((before, value_away))

time: 107 us -> 107 us (level)
  transfers between devices with their start and end apart: 15 -> 15, of which waited for: 7 -> 8; matrix products, arithmetic and copies ran while one was open for 9% -> 9% of each run, Pallas kernels for 21% -> 21%
where the time goes in v5:
time: 107 us
  starting transfers between devices  39.3 us (37%)
  Pallas kernels  29.7 us (28%)
  waiting for transfers between devices  27.8 us (26%)
  other arithmetic  8.39 us (8%)
    all_to_all x1, waiting for transfers between devices, per_device(): lax.all_to_all(back.reshape(images, CAP * words, columns + width), 'dp',...  18 us
    ppermute x13, starting transfers between devices, permute(): return lax.ppermute(values, 'feat', pairs)  16.9 us
    all_to_all x1, starting transfers between devices, per_device(): lax.all_to_all(sent.reshape(images, CAP * words, columns), 'dp', 0, 0, ti...  11.7 us
    all_to_all x1, starting transfers between devices, per_device(): lax.all_to_all(back.reshape(images, CAP * words, columns + width), 'dp',...  10.8 us
    pallas_call x2, Pallas kernels, project(): pl.pallas_call(functools.partial(project_kernel, outs=len(outs)), grid_sp...  10.4 us
    ppermute x13, waiting for transfers between devices, permute(): return lax.ppermute(values, 'feat', pairs)  8.42 us
    pallas_call x2, Pallas kernels, query_step(): pl.pallas_call(functools.partial(query_step_kernel, places=places, first=...  6.96 us
    pallas_call x1, Pallas kernels, attend(): pl.pallas_call(attend_kernel, in_specs=[vmem] * 3, out_specs=vmem, out_sh...  5.71 us
  transfers between devices with their start and end apart: 15, of which 8 were waited for; matrix products, arithmetic and copies ran while one was open for 9% of the time, Pallas kernels for 21%

profile of v5, /device:TPU:1, one launch (start us, length us, event | category | flops | bytes accessed | tf_op | source)
XLA Modules:
  0.0 107.0 jit_solution(1667527345494257366)
XLA Ops:
  0.0 2.0 %collective-permute-start = (bf16[128,1024]{1,0:T(8,128)(2,1)}, bf16[128,1024]{1,0:T(8,128)(2,1)S(1)}, u32[]{:S(2)}, u32[]{:S(2)}) collective-permute-start(bf16[128,1024]{1,0:T(8,128)(2,1)} %param.9), channel_id=1, source_target_pairs={{0,64},{16,80},{32,96},{48,112},{64,0},{80,16},{96,32},{112,48},{1... | collective-permute-start | bytes 786440 | tf_op jit(solution)/shard_map/ppermute | solution.py:23
  2.0 3.3 %project.3 = f32[4,128,1024]{2,1,0:T(8,128)S(1)} custom-call(s32[1]{0:T(128)} %bitcast.mine._, bf16[960,2048]{1,0:T(8,128)(2,1)} %refs_3_.3, bf16[960,2048]{1,0:T(8,128)(2,1)} %refs_3_.3, bf16[960,2048]{1,0:T(8,128)(2,1)} %refs_3_.3, bf16[960,2048]{1,0:T(8,128)(2,1)} %refs_3_.3, bf16[960,1024]{1,0:T(8,128)(2,1)} %bitcast.46), custom_call_target="tpu_custom_call" | custom-call | tf_op jit(solution)/shard_map/project/pallas_call | solution.py:48
  5.4 0.0 copy-start.6
  5.4 1.3 %multiply_convert_fusion = f16[4,128,1024]{2,1,0:T(8,128)(2,1)} fusion(f32[4,128,1024]{2,1,0:T(8,128)S(1)} %project.3), kind=kLoop, calls=%fused_computation | loop fusion | flops 1048576 | bytes 3145728 | tf_op jit(solution)/shard_map/convert_element_type | solution.py:294
  6.6 0.0 collective-permute-start.5
  6.6 1.1 %collective-permute-done = bf16[128,1024]{1,0:T(8,128)(2,1)S(1)} collective-permute-done((bf16[128,1024]{1,0:T(8,128)(2,1)}, bf16[128,1024]{1,0:T(8,128)(2,1)S(1)}, u32[]{:S(2)}, u32[]{:S(2)}) %collective-permute-start) | collective-permute-done | bytes 262176 | tf_op jit(solution)/shard_map/ppermute | solution.py:23
  7.8 0.0 copy-done.6
  7.8 0.1 pad_maximum_fusion.refs_0_
  7.8 1.8 %collective-permute-start.1 = (bf16[2,128,1024]{2,1,0:T(8,128)(2,1)S(1)}, bf16[2,128,1024]{2,1,0:T(8,128)(2,1)S(1)}, u32[]{:S(2)}, u32[]{:S(2)}) collective-permute-start(bf16[2,128,1024]{2,1,0:T(8,128)(2,1)S(1)} %pad_maximum_fusion.refs_0_), channel_id=1, source_target_pairs={{0,16},{16,32},{32,48},{48,0},{64,80},{80,96},{96,112},{112,64},{1... | collective-permute-start | bytes 1572872 | tf_op jit(solution)/shard_map/ppermute | solution.py:23
  9.6 1.5 %collective-permute-start.3 = (bf16[2,128,1024]{2,1,0:T(8,128)(2,1)S(1)}, bf16[2,128,1024]{2,1,0:T(8,128)(2,1)S(1)}, u32[]{:S(2)}, u32[]{:S(2)}) collective-permute-start(bf16[2,128,1024]{2,1,0:T(8,128)(2,1)S(1)} %pad_maximum_fusion.refs_0_), channel_id=1, source_target_pairs={{0,48},{16,0},{32,16},{48,32},{64,112},{80,64},{96,80},{112,96},{1... | collective-permute-start | bytes 1572872 | tf_op jit(solution)/shard_map/ppermute | solution.py:23
  11.2 3.0 %query_step.2.refs_3_ = f32[128,1024]{1,0:T(8,128)S(1)} custom-call(s32[1]{0:T(128)} %bitcast.mine._, bf16[2,128,1024]{2,1,0:T(8,128)(2,1)S(1)} %pad_maximum_fusion.refs_0_, bf16[8192,1024]{1,0:T(8,128)(2,1)} %refs_2_.7), custom_call_target="tpu_custom_call" | custom-call | tf_op jit(solution)/shard_map/query_step/pallas_call | solution.py:107
  14.1 0.0 copy-start.7
  14.1 7.1 %project.2 = (bf16[4,128,1024]{2,1,0:T(8,128)(2,1)}, f32[4,128,1024]{2,1,0:T(8,128)}, f32[4,128,1024]{2,1,0:T(8,128)}) custom-call(s32[1]{0:T(128)} %bitcast.mine._, bf16[960,2048]{1,0:T(8,128)(2,1)} %refs_3_.3, bf16[960,2048]{1,0:T(8,128)(2,1)} %refs_3_.3, bf16[960,2048]{1,0:T(8,128)(2,1)} %refs_3_.3, bf16[960,2048]{1,0:T(8,128)(2,1)} %refs_3_.3, ...), custom_call_target="tpu_custom_call" | custom-call | tf_op jit(solution)/shard_map/project/pallas_call | solution.py:48
  21.2 0.3 collective-permute-done.1.refs_0_
  21.5 0.1 collective-permute-start.2
  21.6 0.0 collective-permute-done.3.refs_1_
  21.6 0.7 slice.72
  22.3 2.6 %collective-permute-start.4 = (bf16[1,128,1024]{2,1,0:T(8,128)(2,1)}, bf16[1,128,1024]{2,1,0:T(8,128)(2,1)S(1)}, u32[]{:S(2)}, u32[]{:S(2)}) collective-permute-start(bf16[1,128,1024]{2,1,0:T(8,128)(2,1)} %slice.72), channel_id=1, source_target_pairs={{0,48},{16,0},{32,16},{48,32},{64,112},{80,64},{96,80},{112,96},{1... | collective-permute-start | bytes 786440 | tf_op jit(solution)/shard_map/ppermute | solution.py:23
  25.0 1.0 collective-permute-start.9
  25.9 0.0 copy-done.7
  25.9 0.1 copy.11.ids_ref
  26.0 0.0 copy-start
  26.0 0.0 copy-start.1
  26.0 4.0 %query_step.3.refs_3_ = f32[128,1024]{1,0:T(8,128)S(1)} custom-call(s32[1]{0:T(128)} %bitcast.mine._, bf16[2,128,1024]{2,1,0:T(8,128)(2,1)S(1)} %collective-permute-done.1.refs_0_, bf16[2,128,1024]{2,1,0:T(8,128)(2,1)S(1)} %collective-permute-done.3.refs_1_, bf16[8192,1024]{1,0:T(8,128)(2,1)} %refs_2_.7, f32[128,1024]{1,0:T(8,128)S(1)} %query_step.2.refs_3_), custom_call_target="tpu_custom_call" | custom-call | tf_op jit(solution)/shard_map/query_step/pallas_call | solution.py:107
  30.0 0.5 collective-permute-done.5
  30.5 0.0 copy-start.4
  30.5 0.0 collective-permute-done.2.refs_0_
  30.5 0.0 collective-permute-done.4.refs_1_
  30.6 0.0 copy-done
  30.6 0.0 copy-done.1
  30.6 0.0 copy-start.2
  30.6 4.9 %query_last.1 = bf16[512,1024]{1,0:T(8,128)(2,1)} custom-call(s32[1]{0:T(128)} %bitcast.mine._, s32[16,2]{1,0:T(8,128)S(1)} %copy.11.ids_ref, s32[16]{0:T(128)S(1)} %copy-done, bf16[1,128,1024]{2,1,0:T(8,128)(2,1)S(1)} %collective-permute-done.2.refs_0_, bf16[1,128,1024]{2,1,0:T(8,128)(2,1)S(1)} %collective-permute-done.4.refs_1_, ...), custom_call_target="tpu_custom_call" | custom-call | tf_op jit(solution)/shard_map/query_last/pallas_call | solution.py:173
  35.5 0.0 copy-done.4
  35.5 0.0 copy-done.2
  35.5 0.0 copy-start.3
  35.5 1.0 fusion.5
  36.6 1.3 %collective-permute-start.6 = (f16[128,1024]{1,0:T(8,128)(2,1)}, f16[128,1024]{1,0:T(8,128)(2,1)S(1)}, u32[]{:S(2)}, u32[]{:S(2)}) collective-permute-start(f16[128,1024]{1,0:T(8,128)(2,1)} %get-tuple-element.30), channel_id=1, source_target_pairs={{0,16},{16,32},{32,48},{48,0},{64,80},{80,96},{96,112},{112,64},{1... | collective-permute-start | bytes 786440 | tf_op jit(solution)/shard_map/ppermute | solution.py:23
  37.9 1.4 %collective-permute-start.7 = (f16[128,1024]{1,0:T(8,128)(2,1)}, f16[128,1024]{1,0:T(8,128)(2,1)}, u32[]{:S(2)}, u32[]{:S(2)}) collective-permute-start(f16[128,1024]{1,0:T(8,128)(2,1)} %get-tuple-element.32), channel_id=1, source_target_pairs={{0,48},{16,0},{32,16},{48,32},{64,112},{80,64},{96,80},{112,96},{1... | collective-permute-start | bytes 786440 | tf_op jit(solution)/shard_map/ppermute | solution.py:23
  39.3 1.6 %collective-permute-start.8 = (f16[128,1024]{1,0:T(8,128)(2,1)}, f16[128,1024]{1,0:T(8,128)(2,1)}, u32[]{:S(2)}, u32[]{:S(2)}) collective-permute-start(f16[128,1024]{1,0:T(8,128)(2,1)} %get-tuple-element.31), channel_id=1, source_target_pairs={{0,32},{16,48},{32,0},{48,16},{64,96},{80,112},{96,64},{112,80},{1... | collective-permute-start | bytes 786440 | tf_op jit(solution)/shard_map/ppermute | solution.py:23
  41.0 11.7 %all-to-all-start = ((bf16[16,32,1024]{2,1,0:T(8,128)(2,1)}), bf16[16,32,1024]{2,1,0:T(8,128)(2,1)S(1)}, u32[]{:S(2)}, u32[]{:S(2)}) async-start(bf16[16,32,1024]{2,1,0:T(8,128)(2,1)} %bitcast.7), calls=%async_computation | async-start | bytes 2097152 | tf_op jit(solution)/shard_map/all_to_all | solution.py:322
  52.6 0.0 copy-start.8
  52.6 0.0 collective-permute-done.6
  52.6 0.0 copy-start.5
  52.6 0.0 collective-permute-done.7
  52.7 0.0 collective-permute-done.8
  52.7 0.0 copy-done.3
  52.7 1.4 %multiply_reduce_fusion = f32[1024]{0:T(1024)S(1)} fusion(f16[128,1024]{1,0:T(8,128)(2,1)} %collective-permute-done.8, f16[128,1024]{1,0:T(8,128)(2,1)} %collective-permute-done.7, f16[128,1024]{1,0:T(8,128)(2,1)S(1)} %collective-permute-done.6, f16[4,128,1024]{2,1,0:T(8,128)(2,1)} %copy-done.4, f32[4,128,1024]{2,1,0:T(8,128)S(1)} %copy-done.3), kind=kLoop, calls=%fused_computation.13 | loop fusion | flops 1440768 | bytes 1576960 | tf_op jit(solution)/shard_map/reduce_sum | solution.py:336
  54.1 0.0 collective-permute-done.9
  54.1 1.8 %fusion.8 = (bf16[128,1024]{1,0:T(8,128)(2,1)S(1)}, bf16[128,1024]{1,0:T(8,128)(2,1)S(1)}, bf16[128,1024]{1,0:T(8,128)(2,1)S(1)}) fusion(f32[4,128,1024]{2,1,0:T(8,128)} %get-tuple-element.25, bf16[4,128,1024]{2,1,0:T(8,128)(2,1)} %collective-permute-done.9), kind=kLoop, calls=%fused_computation.20 | loop fusion | flops 1179648 | bytes 3145728 | tf_op jit(solution)/shard_map/convert_element_type | solution.py:330
  56.0 0.0 copy-done.5
  56.0 0.5 collective-permute-start.10
  56.5 2.3 %collective-permute-start.11 = (bf16[128,1024]{1,0:T(8,128)(2,1)S(1)}, bf16[128,1024]{1,0:T(8,128)(2,1)S(1)}, u32[]{:S(2)}, u32[]{:S(2)}) collective-permute-start(bf16[128,1024]{1,0:T(8,128)(2,1)S(1)} %get-tuple-element.29), channel_id=1, source_target_pairs={{0,48},{16,0},{32,16},{48,32},{64,112},{80,64},{96,80},{112,96},{1... | collective-permute-start | bytes 786440 | tf_op jit(solution)/shard_map/ppermute | solution.py:23
  58.7 0.7 collective-permute-start.12
  59.4 0.0 copy-done.8
  59.4 1.5 %multiply_convert_fusion.1.key_ref = bf16[128,1024]{1,0:T(8,128)(2,1)S(1)} fusion(f32[128]{0:T(128)S(1)} %copy-done.8, f32[1024]{0:T(1024)S(1)} %add_rsqrt_fusion, f16[128,1024]{1,0:T(8,128)(2,1)} %collective-permute-done.8, f16[128,1024]{1,0:T(8,128)(2,1)} %collective-permute-done.7, f16[128,1024]{1,0:T(8,128)(2,1)} %copy-done.5, ...), kind=kLoop, calls=%fused_computation.12 | loop fusion | flops 1572864 | bytes 1839616 | tf_op jit(solution)/shard_map/convert_element_type | solution.py:339
  60.9 2.1 %collective-permute-done.10 = bf16[128,1024]{1,0:T(8,128)(2,1)S(1)} collective-permute-done((bf16[128,1024]{1,0:T(8,128)(2,1)S(1)}, bf16[128,1024]{1,0:T(8,128)(2,1)S(1)}, u32[]{:S(2)}, u32[]{:S(2)}) %collective-permute-start.10) | collective-permute-done | bytes 262176 | tf_op jit(solution)/shard_map/ppermute | solution.py:23
  63.0 2.5 %collective-permute-done.11 = bf16[128,1024]{1,0:T(8,128)(2,1)S(1)} collective-permute-done((bf16[128,1024]{1,0:T(8,128)(2,1)S(1)}, bf16[128,1024]{1,0:T(8,128)(2,1)S(1)}, u32[]{:S(2)}, u32[]{:S(2)}) %collective-permute-start.11) | collective-permute-done | bytes 262176 | tf_op jit(solution)/shard_map/ppermute | solution.py:23
  65.5 1.9 %collective-permute-done.12 = bf16[128,1024]{1,0:T(8,128)(2,1)S(1)} collective-permute-done((bf16[128,1024]{1,0:T(8,128)(2,1)S(1)}, bf16[128,1024]{1,0:T(8,128)(2,1)S(1)}, u32[]{:S(2)}, u32[]{:S(2)}) %collective-permute-start.12) | collective-permute-done | bytes 262176 | tf_op jit(solution)/shard_map/ppermute | solution.py:23
  67.3 1.3 %fusion.2.value_ref = bf16[128,1024]{1,0:T(8,128)(2,1)S(1)} fusion(bf16[128,1024]{1,0:T(8,128)(2,1)S(1)} %collective-permute-done.12, bf16[128,1024]{1,0:T(8,128)(2,1)S(1)} %collective-permute-done.11, bf16[128,1024]{1,0:T(8,128)(2,1)S(1)} %collective-permute-done.10, f32[4,128,1024]{2,1,0:T(8,128)} %get-tuple-element.25, ...), kind=kLoop, calls=%fused_computation.5 | loop fusion | flops 1179648 | bytes 1835008 | tf_op jit(solution)/shard_map/convert_element_type | solution.py:340
  68.6 1.4 %all-to-all-done = bf16[16,32,1024]{2,1,0:T(8,128)(2,1)S(1)} async-done(((bf16[16,32,1024]{2,1,0:T(8,128)(2,1)}), bf16[16,32,1024]{2,1,0:T(8,128)(2,1)S(1)}, u32[]{:S(2)}, u32[]{:S(2)}) %all-to-all-start) | async-done | bytes 1048608 | tf_op jit(solution)/shard_map/all_to_all | solution.py:322
  70.1 5.7 %attend.1 = bf16[512,1152]{1,0:T(8,128)(2,1)} custom-call(bf16[512,1024]{1,0:T(8,128)(2,1)S(1)} %bitcast.44, bf16[128,1024]{1,0:T(8,128)(2,1)S(1)} %multiply_convert_fusion.1.key_ref, bf16[128,1024]{1,0:T(8,128)(2,1)S(1)} %fusion.2.value_ref), custom_call_target="tpu_custom_call" | custom-call | tf_op jit(solution)/shard_map/attend/pallas_call | solution.py:218
  75.8 10.8 %all-to-all-start.1 = ((bf16[16,32,1152]{2,1,0:T(8,128)(2,1)}), bf16[16,32,1152]{2,1,0:T(8,128)(2,1)S(1)}, u32[]{:S(2)}, u32[]{:S(2)}) async-start(bf16[16,32,1152]{2,1,0:T(8,128)(2,1)} %bitcast.17), calls=%async_computation.1 | async-start | bytes 2359296 | tf_op jit(solution)/shard_map/all_to_all | solution.py:343
  87.2 18.0 %all-to-all-done.1 = bf16[16,32,1152]{2,1,0:T(8,128)(2,1)S(1)} async-done(((bf16[16,32,1152]{2,1,0:T(8,128)(2,1)}), bf16[16,32,1152]{2,1,0:T(8,128)(2,1)S(1)}, u32[]{:S(2)}, u32[]{:S(2)}) %all-to-all-start.1) | async-done | bytes 1179680 | tf_op jit(solution)/shard_map/all_to_all | solution.py:343
  105.2 1.8 %combine.1 = bf16[128,1024]{1,0:T(8,128)(2,1)} custom-call(s32[16,2]{1,0:T(8,128)S(1)} %copy.11.ids_ref, s32[16]{0:T(128)S(1)} %copy-done, bf16[512,1152]{1,0:T(8,128)(2,1)S(1)} %bitcast.43, f32[1,128]{1,0:T(1,128)S(1)} %broadcast_in_dim.15.gate_ref), custom_call_target="tpu_custom_call" | custom-call | tf_op jit(solution)/shard_map/combine/pallas_call | solution.py:263
  (3 shorter events, 0.0 us)
Async XLA Ops:
  0.0 7.8 %collective-permute-start = (bf16[128,1024]{1,0:T(8,128)(2,1)}, bf16[128,1024]{1,0:T(8,128)(2,1)S(1)}, u32[]{:S(2)}, u32[]{:S(2)}) collective-permute-start(bf16[128,1024]{1,0:T(8,128)(2,1)} %param.9), channel_id=1, source_target_pairs={{0,64},{16,80},{32,96},{48,112},{64,0},{80,16},{96,32},{112,48},{1... | collective-permute-start | bytes 786440 | tf_op jit(solution)/shard_map/ppermute | solution.py:23
  5.4 2.4 %copy-start.6 = (bf16[128,1024]{1,0:T(8,128)(2,1)S(1)}, bf16[128,1024]{1,0:T(8,128)(2,1)}, u32[]{:S(2)}) copy-start(bf16[128,1024]{1,0:T(8,128)(2,1)} %param.9) | copy-start | bytes 786436
  6.6 23.9 %collective-permute-start.5 = (f16[4,128,1024]{2,1,0:T(8,128)(2,1)}, f16[4,128,1024]{2,1,0:T(8,128)(2,1)S(1)}, u32[]{:S(2)}, u32[]{:S(2)}) collective-permute-start(f16[4,128,1024]{2,1,0:T(8,128)(2,1)} %multiply_convert_fusion), channel_id=1, source_target_pairs={{0,64},{16,80},{32,96},{48,112},{64,0},{80,16},{96,32},{112,48},{1... | collective-permute-start | bytes 3145736 | tf_op jit(solution)/shard_map/ppermute | solution.py:23
  7.8 13.6 %collective-permute-start.1 = (bf16[2,128,1024]{2,1,0:T(8,128)(2,1)S(1)}, bf16[2,128,1024]{2,1,0:T(8,128)(2,1)S(1)}, u32[]{:S(2)}, u32[]{:S(2)}) collective-permute-start(bf16[2,128,1024]{2,1,0:T(8,128)(2,1)S(1)} %pad_maximum_fusion.refs_0_), channel_id=1, source_target_pairs={{0,16},{16,32},{32,48},{48,0},{64,80},{80,96},{96,112},{112,64},{1... | collective-permute-start | bytes 1572872 | tf_op jit(solution)/shard_map/ppermute | solution.py:23
  9.6 12.0 %collective-permute-start.3 = (bf16[2,128,1024]{2,1,0:T(8,128)(2,1)S(1)}, bf16[2,128,1024]{2,1,0:T(8,128)(2,1)S(1)}, u32[]{:S(2)}, u32[]{:S(2)}) collective-permute-start(bf16[2,128,1024]{2,1,0:T(8,128)(2,1)S(1)} %pad_maximum_fusion.refs_0_), channel_id=1, source_target_pairs={{0,48},{16,0},{32,16},{48,32},{64,112},{80,64},{96,80},{112,96},{1... | collective-permute-start | bytes 1572872 | tf_op jit(solution)/shard_map/ppermute | solution.py:23
  14.1 11.8 %copy-start.7 = (s32[16,2]{0,1:T(2,128)S(1)}, s32[16,2]{0,1:T(2,128)}, u32[]{:S(2)}) copy-start(s32[16,2]{0,1:T(2,128)} %param.16) | copy-start | bytes 388
  21.5 9.1 %collective-permute-start.2 = (bf16[1,128,1024]{2,1,0:T(8,128)(2,1)S(1)}, bf16[1,128,1024]{2,1,0:T(8,128)(2,1)S(1)}, u32[]{:S(2)}, u32[]{:S(2)}) collective-permute-start(bf16[1,128,1024]{2,1,0:T(8,128)(2,1)S(1)} %slice.54), channel_id=1, source_target_pairs={{0,16},{16,32},{32,48},{48,0},{64,80},{80,96},{96,112},{112,64},{1... | collective-permute-start | bytes 786440 | tf_op jit(solution)/shard_map/ppermute | solution.py:23
  22.3 8.2 %collective-permute-start.4 = (bf16[1,128,1024]{2,1,0:T(8,128)(2,1)}, bf16[1,128,1024]{2,1,0:T(8,128)(2,1)S(1)}, u32[]{:S(2)}, u32[]{:S(2)}) collective-permute-start(bf16[1,128,1024]{2,1,0:T(8,128)(2,1)} %slice.72), channel_id=1, source_target_pairs={{0,48},{16,0},{32,16},{48,32},{64,112},{80,64},{96,80},{112,96},{1... | collective-permute-start | bytes 786440 | tf_op jit(solution)/shard_map/ppermute | solution.py:23
  25.0 29.2 %collective-permute-start.9 = (bf16[4,128,1024]{2,1,0:T(8,128)(2,1)}, bf16[4,128,1024]{2,1,0:T(8,128)(2,1)}, u32[]{:S(2)}, u32[]{:S(2)}) collective-permute-start(bf16[4,128,1024]{2,1,0:T(8,128)(2,1)} %get-tuple-element.26), channel_id=1, source_target_pairs={{0,64},{16,80},{32,96},{48,112},{64,0},{80,16},{96,32},{112,48},{1... | collective-permute-start | bytes 3145736 | tf_op jit(solution)/shard_map/ppermute | solution.py:23
  26.0 4.6 %copy-start = (s32[16]{0:T(128)S(1)}, s32[16]{0:T(128)}, u32[]{:S(2)}) copy-start(s32[16]{0:T(128)} %slots_ref.3) | copy-start | bytes 196
  26.0 4.6 %copy-start.1 = (f32[128]{0:T(128)S(1)}, f32[128]{0:T(128)}, u32[]{:S(2)}) copy-start(f32[128]{0:T(128)} %param.13) | copy-start | bytes 1540
  30.5 5.0 %copy-start.4 = (f16[4,128,1024]{2,1,0:T(8,128)(2,1)}, f16[4,128,1024]{2,1,0:T(8,128)(2,1)S(1)}, u32[]{:S(2)}) copy-start(f16[4,128,1024]{2,1,0:T(8,128)(2,1)S(1)} %collective-permute-done.5) | copy-start | bytes 3145732
  30.6 4.9 %copy-start.2 = (f32[4,128,1024]{2,1,0:T(8,128)S(1)}, f32[4,128,1024]{2,1,0:T(8,128)}, u32[]{:S(2)}) copy-start(f32[4,128,1024]{2,1,0:T(8,128)} %get-tuple-element.23) | copy-start | bytes 6291460
  35.5 17.2 %copy-start.3 = (f32[4,128,1024]{2,1,0:T(8,128)S(1)}, f32[4,128,1024]{2,1,0:T(8,128)}, u32[]{:S(2)}) copy-start(f32[4,128,1024]{2,1,0:T(8,128)} %get-tuple-element.23) | copy-start | bytes 6291460
  36.6 16.1 %collective-permute-start.6 = (f16[128,1024]{1,0:T(8,128)(2,1)}, f16[128,1024]{1,0:T(8,128)(2,1)S(1)}, u32[]{:S(2)}, u32[]{:S(2)}) collective-permute-start(f16[128,1024]{1,0:T(8,128)(2,1)} %get-tuple-element.30), channel_id=1, source_target_pairs={{0,16},{16,32},{32,48},{48,0},{64,80},{80,96},{96,112},{112,64},{1... | collective-permute-start | bytes 786440 | tf_op jit(solution)/shard_map/ppermute | solution.py:23
  37.9 14.8 %collective-permute-start.7 = (f16[128,1024]{1,0:T(8,128)(2,1)}, f16[128,1024]{1,0:T(8,128)(2,1)}, u32[]{:S(2)}, u32[]{:S(2)}) collective-permute-start(f16[128,1024]{1,0:T(8,128)(2,1)} %get-tuple-element.32), channel_id=1, source_target_pairs={{0,48},{16,0},{32,16},{48,32},{64,112},{80,64},{96,80},{112,96},{1... | collective-permute-start | bytes 786440 | tf_op jit(solution)/shard_map/ppermute | solution.py:23
  39.3 13.4 %collective-permute-start.8 = (f16[128,1024]{1,0:T(8,128)(2,1)}, f16[128,1024]{1,0:T(8,128)(2,1)}, u32[]{:S(2)}, u32[]{:S(2)}) collective-permute-start(f16[128,1024]{1,0:T(8,128)(2,1)} %get-tuple-element.31), channel_id=1, source_target_pairs={{0,32},{16,48},{32,0},{48,16},{64,96},{80,112},{96,64},{112,80},{1... | collective-permute-start | bytes 786440 | tf_op jit(solution)/shard_map/ppermute | solution.py:23
  41.0 29.1 %all-to-all-start = ((bf16[16,32,1024]{2,1,0:T(8,128)(2,1)}), bf16[16,32,1024]{2,1,0:T(8,128)(2,1)S(1)}, u32[]{:S(2)}, u32[]{:S(2)}) async-start(bf16[16,32,1024]{2,1,0:T(8,128)(2,1)} %bitcast.7), calls=%async_computation | async-start | bytes 2097152 | tf_op jit(solution)/shard_map/all_to_all | solution.py:322
  52.6 6.8 %copy-start.8 = (f32[128]{0:T(128)S(1)}, f32[128]{0:T(128)}, u32[]{:S(2)}) copy-start(f32[128]{0:T(128)} %param.14) | copy-start | bytes 1540
  52.6 3.3 %copy-start.5 = (f16[128,1024]{1,0:T(8,128)(2,1)}, f16[128,1024]{1,0:T(8,128)(2,1)S(1)}, u32[]{:S(2)}) copy-start(f16[128,1024]{1,0:T(8,128)(2,1)S(1)} %collective-permute-done.6) | copy-start | bytes 786436
  56.0 7.0 %collective-permute-start.10 = (bf16[128,1024]{1,0:T(8,128)(2,1)S(1)}, bf16[128,1024]{1,0:T(8,128)(2,1)S(1)}, u32[]{:S(2)}, u32[]{:S(2)}) collective-permute-start(bf16[128,1024]{1,0:T(8,128)(2,1)S(1)} %get-tuple-element.27), channel_id=1, source_target_pairs={{0,16},{16,32},{32,48},{48,0},{64,80},{80,96},{96,112},{112,64},{1... | collective-permute-start | bytes 786440 | tf_op jit(solution)/shard_map/ppermute | solution.py:23
  56.5 9.0 %collective-permute-start.11 = (bf16[128,1024]{1,0:T(8,128)(2,1)S(1)}, bf16[128,1024]{1,0:T(8,128)(2,1)S(1)}, u32[]{:S(2)}, u32[]{:S(2)}) collective-permute-start(bf16[128,1024]{1,0:T(8,128)(2,1)S(1)} %get-tuple-element.29), channel_id=1, source_target_pairs={{0,48},{16,0},{32,16},{48,32},{64,112},{80,64},{96,80},{112,96},{1... | collective-permute-start | bytes 786440 | tf_op jit(solution)/shard_map/ppermute | solution.py:23
  58.7 8.6 %collective-permute-start.12 = (bf16[128,1024]{1,0:T(8,128)(2,1)S(1)}, bf16[128,1024]{1,0:T(8,128)(2,1)S(1)}, u32[]{:S(2)}, u32[]{:S(2)}) collective-permute-start(bf16[128,1024]{1,0:T(8,128)(2,1)S(1)} %get-tuple-element.28), channel_id=1, source_target_pairs={{0,32},{16,48},{32,0},{48,16},{64,96},{80,112},{96,64},{112,80},{1... | collective-permute-start | bytes 786440 | tf_op jit(solution)/shard_map/ppermute | solution.py:23
  75.8 29.4 %all-to-all-start.1 = ((bf16[16,32,1152]{2,1,0:T(8,128)(2,1)}), bf16[16,32,1152]{2,1,0:T(8,128)(2,1)S(1)}, u32[]{:S(2)}, u32[]{:S(2)}) async-start(bf16[16,32,1152]{2,1,0:T(8,128)(2,1)} %bitcast.17), calls=%async_computation.1 | async-start | bytes 2359296 | tf_op jit(solution)/shard_map/all_to_all | solution.py:343
